TPU v7x, 32 devices: a whole 2x2x4 slice. The times are simulated.
32 devices in a mesh: blk: 4 (over x, core), uly: 8 (over z, y).
Axes of the slice: x: 2, y: 2, z: 4, core: 2. Of those that a mesh axis runs over, the one named last changes fastest.
Arguments:
- residual: bfloat16 [2, 2048, 1024], P(None, ('uly', 'blk')), may hold values from -6 to 6
- cotangent: bfloat16 [2, 2048, 1024], P(None, ('uly', 'blk')), may hold values from -6 to 6
- lengths: int32 [2], replicated, may hold values from 512 to 2048, as said below
- positions: int32 [2, 2048], P(None, ('uly', 'blk')), may hold values from 0 to 2047, as said below
- masters: float32 [12596224], P(('blk', 'uly')), may hold values from -2 to 2
- momenta: float32 [12596224], P(('blk', 'uly')), may hold values from -102.4 to 102.4
- averages: float32 [12596224], P(('blk', 'uly')), may hold values from -2 to 2
Outputs:
- block_output: bfloat16 [2, 2048, 1024], P(None, ('uly', 'blk'))
- input_gradient: bfloat16 [2, 2048, 1024], P(None, ('uly', 'blk'))
- gradients: float32 [12596224], P(('blk', 'uly'))
- updated_masters: float32 [12596224], P(('blk', 'uly'))
- updated_momenta: float32 [12596224], P(('blk', 'uly'))
- updated_averages: float32 [12596224], P(('blk', 'uly'))
Inputs may be any that keep to these rules, and one draw needn't show every extreme that they name: `lengths`: in every draw some slot is live over all 2048 positions; tokens at or past a slot's length are padding. Each slot's positions start at 0, restart at 0 at the first token of each packed document, and otherwise rise by one per token; the first slot holds a single document, every other slot two or more.
All inputs are finite; a program needn't handle non-finite values.
Results may differ from a plain program's by a relative error of at most 0.014.
The roundings to bfloat16 on the way count: a program that leaves them out, or rounds other values in their place, can miss the bound.
Values may be sent and summed in bfloat16 or wider, within the bound.
No kernel may reach another device: no remote copies, remote signals or barrier semaphores. Data moves between devices by JAX's collectives and lax.ppermute only.
A program may use at most 256 MiB of HBM per device.

v0:
```python
from functools import partial
import math

import jax
import jax.numpy as jnp
from jax import lax
from jax.experimental import pallas as pl
from jax.experimental.pallas import tpu as pltpu
from jax.sharding import Mesh, PartitionSpec as P

D = 1024
H = 16
HD = 64
ROT = 16
FF = 4096


EPSILON = 1e-05
NEGATIVE = -1e30
MOMENTUM = 0.5
LEARN_RATE = 0.05
AVERAGE_DECAY = 0.5
ROTARY_BASE = 10000.0


def passed_along(block, axis, distance):
    devices = range(lax.axis_size(axis))
    route = [((i - distance) % len(devices), i) for i in devices]
    return lax.ppermute(block, axis, route)


def unpack(flat_vector):
    layouts = [
        (D,),
        (D,),
        (D,),
        (D,),
        (D, 3 * D),
        (3 * D,),
        (D, D),
        (D,),
        (D, FF),
        (FF,),
        (FF, D),
        (D,),
    ]
    pieces = []
    cursor = 0
    for layout in layouts:
        number = math.prod(layout)
        pieces.append(flat_vector[cursor : cursor + number].reshape(layout))
        cursor += number
    return pieces


def layer_norm(values, gain, shift):
    centered = values - jnp.mean(values, axis=-1, keepdims=True)
    variance = jnp.mean(centered * centered, axis=-1, keepdims=True)
    return centered * lax.rsqrt(variance + EPSILON) * gain + shift


def rotary_tables(positions):
    half_dims = ROT // 2
    inverse = ROTARY_BASE ** (-(jnp.arange(half_dims, dtype=jnp.float32) * 2.0 / ROT))
    angles = positions.astype(jnp.float32)[..., None] * inverse
    return (jnp.cos(angles), jnp.sin(angles))


def rotate(values, cos_table, sin_table):
    half_dims = ROT // 2
    first_half = values[..., :half_dims]
    second_half = values[..., half_dims:ROT]
    return jnp.concatenate(
        [
            first_half * cos_table - second_half * sin_table,
            second_half * cos_table + first_half * sin_table,
            values[..., ROT:],
        ],
        axis=-1,
    )


def group_tokens(source, group_count, uly_count, span_rows):
    spans = jnp.arange(uly_count, dtype=jnp.int32)[:, None] * group_count + source
    return (spans * span_rows + jnp.arange(span_rows, dtype=jnp.int32)[None, :]).reshape(-1)


def block_scores(queries, keys_rows, row_tokens, col_tokens, length):
    scores = jnp.einsum(
        "qhd,khd->hqk", queries, keys_rows, preferred_element_type=jnp.float32
    ) * HD ** (-0.5)
    allowed = (col_tokens[None, :] <= row_tokens[:, None]) & (col_tokens[None, :] < length)
    return jnp.where(allowed[None], scores, NEGATIVE)


def is_live(row_tokens, col_tokens, length):
    return (col_tokens[0] <= row_tokens[-1]) & (col_tokens[0] < length)


def fold_stats(row_max, row_total, queries, key_value, lengths, row_tokens, col_tokens):

    def per_slot(inputs):
        slot_max, slot_total, slot_queries, slot_pairs, length = inputs

        def compute(current):
            prev_max, prev_total = current
            scores = block_scores(slot_queries, slot_pairs[:, :, 0], row_tokens, col_tokens, length)
            next_max = jnp.maximum(prev_max, jnp.max(scores, axis=-1))
            next_total = prev_total * jnp.exp(prev_max - next_max) + jnp.sum(
                jnp.exp(scores - next_max[..., None]), axis=-1
            )
            return (next_max, next_total)

        return lax.cond(
            is_live(row_tokens, col_tokens, length),
            compute,
            lambda current: current,
            (slot_max, slot_total),
        )

    return lax.map(per_slot, (row_max, row_total, queries, key_value, lengths))


def fold_values(attended, queries, key_value, log_total, lengths, row_tokens, col_tokens):

    def per_slot(inputs):
        slot_out, slot_queries, slot_pairs, slot_log, length = inputs

        def compute(current):
            scores = block_scores(slot_queries, slot_pairs[:, :, 0], row_tokens, col_tokens, length)
            prob_low = jnp.exp(scores - slot_log[..., None]).astype(jnp.bfloat16)
            return current + jnp.einsum(
                "hqk,khd->qhd", prob_low, slot_pairs[:, :, 1], preferred_element_type=jnp.float32
            )

        return lax.cond(
            is_live(row_tokens, col_tokens, length), compute, lambda current: current, slot_out
        )

    return lax.map(per_slot, (attended, queries, key_value, log_total, lengths))


def fold_grads(
    query_grad,
    pair_grad,
    queries,
    key_value,
    grad_out,
    log_total,
    row_delta,
    lengths,
    row_tokens,
    col_tokens,
):

    def per_slot(inputs):
        (
            slot_qgrad,
            slot_pgrad,
            slot_queries,
            slot_pairs,
            slot_gout,
            slot_log,
            slot_delta,
            length,
        ) = inputs

        def compute(current):
            cur_qgrad, cur_pgrad = current
            scores = block_scores(slot_queries, slot_pairs[:, :, 0], row_tokens, col_tokens, length)
            attend_prob = jnp.exp(scores - slot_log[..., None])
            prob_low = attend_prob.astype(jnp.bfloat16)
            prob_grad = jnp.einsum(
                "qhd,khd->hqk", slot_gout, slot_pairs[:, :, 1], preferred_element_type=jnp.float32
            )
            score_grad = (attend_prob * (prob_grad - slot_delta[..., None])).astype(jnp.bfloat16)
            cur_qgrad = cur_qgrad + jnp.einsum(
                "hqk,khd->qhd", score_grad, slot_pairs[:, :, 0], preferred_element_type=jnp.float32
            ) * HD ** (-0.5)
            key_grad = jnp.einsum(
                "hqk,qhd->khd", score_grad, slot_queries, preferred_element_type=jnp.float32
            ) * HD ** (-0.5)
            value_grad = jnp.einsum(
                "hqk,qhd->khd", prob_low, slot_gout, preferred_element_type=jnp.float32
            )
            return (cur_qgrad, cur_pgrad + jnp.stack([key_grad, value_grad], axis=2))

        return lax.cond(
            is_live(row_tokens, col_tokens, length),
            compute,
            lambda current: current,
            (slot_qgrad, slot_pgrad),
        )

    return lax.map(
        per_slot,
        (query_grad, pair_grad, queries, key_value, grad_out, log_total, row_delta, lengths),
    )


def local(residual, cotangent, lengths, positions, masters, momenta, averages):
    slot_count, span_rows, model_width = residual.shape
    group_count = lax.axis_size("blk")
    uly_count = lax.axis_size("uly")
    group_index = lax.axis_index("blk")
    uly_index = lax.axis_index("uly")
    block_rows = uly_count * span_rows
    full_rows = group_count * block_rows
    local_heads = H // uly_count
    token_rows = slot_count * span_rows
    row_tokens = group_tokens(group_index, group_count, uly_count, span_rows)

    def tokens_of(source):
        return group_tokens(source, group_count, uly_count, span_rows)

    gathered = lax.all_gather(masters.astype(jnp.bfloat16), ("blk", "uly"), axis=0, tiled=True)
    (
        gain_one,
        shift_one,
        gain_two,
        shift_two,
        project_w,
        project_b,
        dense_w,
        dense_b,
        expand_w,
        expand_b,
        shrink_w,
        shrink_b,
    ) = unpack(gathered)
    values = residual.astype(jnp.float32).reshape(token_rows, model_width)
    normed_one, norm_back_one = jax.vjp(
        layer_norm, values, gain_one.astype(jnp.float32), shift_one.astype(jnp.float32)
    )
    normed_two, norm_back_two = jax.vjp(
        layer_norm, values, gain_two.astype(jnp.float32), shift_two.astype(jnp.float32)
    )
    normed_one = normed_one.astype(jnp.bfloat16)
    normed_two = normed_two.astype(jnp.bfloat16)
    mixed_rows = jnp.dot(
        normed_one, project_w, preferred_element_type=jnp.float32
    ) + project_b.astype(jnp.float32)
    mixed_rows = mixed_rows.reshape(slot_count, span_rows, H, 3, HD)
    cos_table, sin_table = rotary_tables(positions)
    cos_table = cos_table[:, :, None, None, :]
    sin_table = sin_table[:, :, None, None, :]
    turned, turn_back = jax.vjp(
        lambda pair_rows: rotate(pair_rows, cos_table, sin_table), mixed_rows[:, :, :, 0:2]
    )
    packed = jnp.concatenate([turned, mixed_rows[:, :, :, 2:3]], axis=3).astype(jnp.bfloat16)
    packed = packed.reshape(slot_count, span_rows, 3 * model_width)
    heads_rows = lax.all_to_all(packed, "uly", split_axis=2, concat_axis=1, tiled=True).reshape(
        slot_count, block_rows, local_heads, 3, HD
    )
    queries = heads_rows[:, :, :, 0]
    key_value = heads_rows[:, :, :, 1:3]
    row_max = jnp.full((slot_count, local_heads, block_rows), NEGATIVE, jnp.float32)
    row_total = jnp.zeros((slot_count, local_heads, block_rows), jnp.float32)
    attended = jnp.zeros((slot_count, block_rows, local_heads, HD), jnp.float32)
    last_tokens = tokens_of((group_index + 1) % group_count)

    def stats_turn(turn_index, carried):
        pairs_now, cur_max, cur_total = carried
        col_tokens = tokens_of((group_index - turn_index) % group_count)
        cur_max, cur_total = fold_stats(
            cur_max, cur_total, queries, pairs_now, lengths, row_tokens, col_tokens
        )
        pairs_now = passed_along(pairs_now, "blk", 1)
        return (pairs_now, cur_max, cur_total)

    pairs_now, row_max, row_total = lax.fori_loop(
        0, group_count - 1, stats_turn, (key_value, row_max, row_total)
    )
    row_max, row_total = fold_stats(
        row_max, row_total, queries, pairs_now, lengths, row_tokens, last_tokens
    )
    log_total = row_max + jnp.log(row_total)

    def value_turn(turn_index, carried):
        pairs_now, cur_out = carried
        col_tokens = tokens_of((group_index - turn_index) % group_count)
        cur_out = fold_values(
            cur_out, queries, pairs_now, log_total, lengths, row_tokens, col_tokens
        )
        pairs_now = passed_along(pairs_now, "blk", 1)
        return (pairs_now, cur_out)

    pairs_now, attended = lax.fori_loop(0, group_count - 1, value_turn, (key_value, attended))
    attended = fold_values(
        attended, queries, pairs_now, log_total, lengths, row_tokens, last_tokens
    )
    heads_out = attended.astype(jnp.bfloat16).reshape(slot_count, block_rows, local_heads * HD)
    merged = lax.all_to_all(heads_out, "uly", split_axis=1, concat_axis=2, tiled=True).reshape(
        token_rows, model_width
    )
    branch_attn = jnp.dot(merged, dense_w, preferred_element_type=jnp.float32) + dense_b.astype(
        jnp.float32
    )
    hidden_pre = jnp.dot(
        normed_two, expand_w, preferred_element_type=jnp.float32
    ) + expand_b.astype(jnp.float32)
    activated, gelu_back = jax.vjp(partial(jax.nn.gelu, approximate=False), hidden_pre)
    activated_low = activated.astype(jnp.bfloat16)
    branch_feed = jnp.dot(
        activated_low, shrink_w, preferred_element_type=jnp.float32
    ) + shrink_b.astype(jnp.float32)
    outputs = (
        (values + branch_attn + branch_feed)
        .astype(jnp.bfloat16)
        .reshape(slot_count, span_rows, model_width)
    )
    first_token = (uly_index * group_count + group_index) * span_rows
    token_index = first_token + jnp.arange(span_rows, dtype=jnp.int32)
    live_mask = (token_index[None, :] < lengths[:, None]).astype(jnp.float32)
    seed_grad = (cotangent.astype(jnp.float32) * live_mask[:, :, None]).reshape(
        token_rows, model_width
    )
    seed_low = seed_grad.astype(jnp.bfloat16)
    dense_w_grad = jnp.einsum("ra,rb->ab", merged, seed_low, preferred_element_type=jnp.float32)
    bias_grad = jnp.sum(seed_low.astype(jnp.float32), axis=0)
    merged_grad = jnp.einsum(
        "rb,ab->ra", seed_low, dense_w, preferred_element_type=jnp.float32
    ).astype(jnp.bfloat16)
    shrink_w_grad = jnp.einsum(
        "rf,rb->fb", activated_low, seed_low, preferred_element_type=jnp.float32
    )
    activated_grad = jnp.einsum("rb,fb->rf", seed_low, shrink_w, preferred_element_type=jnp.float32)
    hidden_grad = gelu_back(activated_grad)[0].astype(jnp.bfloat16)
    expand_w_grad = jnp.einsum(
        "ra,rf->af", normed_two, hidden_grad, preferred_element_type=jnp.float32
    )
    expand_b_grad = jnp.sum(hidden_grad.astype(jnp.float32), axis=0)
    normed_two_grad = jnp.einsum(
        "rf,af->ra", hidden_grad, expand_w, preferred_element_type=jnp.float32
    )
    grad_heads = lax.all_to_all(
        merged_grad.reshape(slot_count, span_rows, model_width),
        "uly",
        split_axis=2,
        concat_axis=1,
        tiled=True,
    )
    grad_out = grad_heads.reshape(slot_count, block_rows, local_heads, HD)
    row_delta = jnp.sum(grad_out.astype(jnp.float32) * attended, axis=-1).transpose(0, 2, 1)
    query_grad = jnp.zeros((slot_count, block_rows, local_heads, HD), jnp.float32)
    pair_grad = jnp.zeros((slot_count, block_rows, local_heads, 2, HD), jnp.float32)

    def grad_turn(turn_index, carried):
        pairs_now, cur_pgrad, cur_qgrad = carried
        col_tokens = tokens_of((group_index - turn_index) % group_count)
        cur_qgrad, cur_pgrad = fold_grads(
            cur_qgrad,
            cur_pgrad,
            queries,
            pairs_now,
            grad_out,
            log_total,
            row_delta,
            lengths,
            row_tokens,
            col_tokens,
        )
        pairs_now = passed_along(pairs_now, "blk", 1)
        cur_pgrad = passed_along(cur_pgrad.astype(jnp.bfloat16), "blk", 1).astype(cur_pgrad.dtype)
        return (pairs_now, cur_pgrad, cur_qgrad)

    pairs_now, pair_grad, query_grad = lax.fori_loop(
        0, group_count - 1, grad_turn, (key_value, pair_grad, query_grad)
    )
    query_grad, pair_grad = fold_grads(
        query_grad,
        pair_grad,
        queries,
        pairs_now,
        grad_out,
        log_total,
        row_delta,
        lengths,
        row_tokens,
        last_tokens,
    )
    pair_grad = passed_along(pair_grad.astype(jnp.bfloat16), "blk", 1).astype(pair_grad.dtype)
    back_packed = jnp.concatenate(
        [query_grad.astype(jnp.bfloat16)[:, :, :, None], pair_grad.astype(jnp.bfloat16)], axis=3
    )
    back_packed = back_packed.reshape(slot_count, block_rows, local_heads * 3 * HD)
    token_grads = lax.all_to_all(
        back_packed, "uly", split_axis=1, concat_axis=2, tiled=True
    ).reshape(slot_count, span_rows, H, 3, HD)
    turned_grad = turn_back(token_grads[:, :, :, 0:2].astype(jnp.float32))[0]
    mixed_grad = jnp.concatenate(
        [turned_grad, token_grads[:, :, :, 2:3].astype(jnp.float32)], axis=3
    ).astype(jnp.bfloat16)
    mixed_grad = mixed_grad.reshape(token_rows, 3 * model_width)
    project_w_grad = jnp.einsum(
        "ra,rc->ac", normed_one, mixed_grad, preferred_element_type=jnp.float32
    )
    project_b_grad = jnp.sum(mixed_grad.astype(jnp.float32), axis=0)
    normed_one_grad = jnp.einsum(
        "rc,ac->ra", mixed_grad, project_w, preferred_element_type=jnp.float32
    )
    values_one, gain_one_grad, shift_one_grad = norm_back_one(normed_one_grad)
    values_two, gain_two_grad, shift_two_grad = norm_back_two(normed_two_grad)
    input_grad = (
        (seed_grad + values_one + values_two)
        .astype(jnp.bfloat16)
        .reshape(slot_count, span_rows, model_width)
    )
    local_grads = jnp.concatenate(
        [
            gain_one_grad,
            shift_one_grad,
            gain_two_grad,
            shift_two_grad,
            project_w_grad.reshape(-1),
            project_b_grad,
            dense_w_grad.reshape(-1),
            bias_grad,
            expand_w_grad.reshape(-1),
            expand_b_grad,
            shrink_w_grad.reshape(-1),
            bias_grad,
        ]
    )
    gradients = lax.psum_scatter(local_grads, ("blk", "uly"), scatter_dimension=0, tiled=True)
    velocity = MOMENTUM * momenta + gradients
    step_rate = LEARN_RATE / math.sqrt(slot_count * full_rows)
    updated = masters - step_rate * (gradients + MOMENTUM * velocity)
    averaged = AVERAGE_DECAY * averages + (1.0 - AVERAGE_DECAY) * updated
    return (outputs, input_grad, gradients, updated, velocity, averaged)


LANES = 128
BLOCK = 256
RING = ("core", "z", "y")
ALL = ("x", "core", "z", "y")
F32 = jnp.float32
BF16 = jnp.bfloat16


def call(body, grid, in_specs, out_specs, out_shape, scratch=(), prefetch=0):
    return pl.pallas_call(
        body,
        grid_spec=pltpu.PrefetchScalarGridSpec(
            num_scalar_prefetch=prefetch,
            grid=grid,
            in_specs=in_specs,
            out_specs=out_specs,
            scratch_shapes=scratch,
        ),
        out_shape=out_shape,
        compiler_params=pltpu.CompilerParams(vmem_limit_bytes=56 << 20),
    )


def whole(shape):
    return pl.BlockSpec(shape, lambda *_: (0,) * len(shape))


def shaped(shape, kind):
    return jax.ShapeDtypeStruct(shape, kind)


def mm(a, b, dims=((1,), (0,))):
    return lax.dot_general(a, b, (dims, ((), ())), preferred_element_type=F32)


def low_lanes(shape):
    return lax.broadcasted_iota(jnp.int32, shape, len(shape) - 1) < LANES // 2


def swap(a):
    return pltpu.roll(a, LANES // 2, 1)


def join(a, a_half, b, b_half):
    first = swap(a) if a_half else a
    second = b if b_half else swap(b)
    return jnp.where(low_lanes(a.shape), first, second)


OWNERS = 32
PER = (3 * D + D + FF + FF) // OWNERS
FLAT = PER * D // LANES
PIECE = FLAT // 16
LEAD = 4 * D // LANES
EDGE = PER * D + 13 * D // OWNERS
PROJECT, PLAIN, PLAIN_EXPAND, EXPAND, EXPAND_PLAIN = range(5)


def plain_place(row, base, count):
    local = row - base
    half = int(local >= count // 2)
    return local - half * (count // 2), half


def dense_place(row):
    if row < 768:
        c = 8 + row // 384
        return (c, 0) + plain_place(row, 384 * (c - 8), 384)
    return (10, 0) + plain_place(row, 768, 256)


def shrink_place(row):
    if row < 256:
        return (21, 64) + plain_place(row, 0, 256)
    c = 22 + (row - 256) // 384
    return (c, 0) + plain_place(row, 256 + 384 * (c - 22), 384)


def expand_places():
    places = [(10, 128, 0, 32)]
    places += [(c, 0, 32 + 96 * (c - 11), 96) for c in range(11, 21)]
    places += [(21, 0, 992, 32)]
    return places


def shifted_rows(source, start, shift, at, rows):
    turn = (LANES - shift) % LANES
    first = pltpu.roll(source[pl.ds(start + at, rows), :], turn, 1)
    second = pltpu.roll(source[pl.ds(start + at + 1, rows), :], turn, 1)
    lane = lax.broadcasted_iota(jnp.int32, (rows, LANES), 1)
    return jnp.where(lane < LANES - shift, first, second)


SHIFT_ROWS = 3200
SEND_ROWS = PIECE + 32 + 16
OWN_ROW = 64


def weights_out_body(scalars, before, own, after, places, out, source, flat, tail):
    start, shift, kind, vector_row = scalars[0], scalars[1], scalars[2], scalars[3]
    count = own.shape[0]
    source[0 : OWN_ROW - 8] = jnp.zeros((OWN_ROW - 8, LANES), F32)
    source[OWN_ROW - 8 : OWN_ROW] = before[...]

    def copy(step, carry):
        at = pl.multiple_of(step * 88, 8)
        source[pl.ds(at + OWN_ROW, 88), :] = own[pl.ds(at, 88), :]
        return carry

    lax.fori_loop(0, count // 88, copy, 0)
    last = OWN_ROW + EDGE // LANES
    source[OWN_ROW + count :] = jnp.zeros((source.shape[0] - OWN_ROW - count, LANES), F32)
    edge = EDGE % LANES
    tail[...] = jnp.zeros(tail.shape, F32)
    tail[7:8] = source[last : last + 1]
    tail[8:40] = pltpu.roll(after[...], edge, 1)
    lane = lax.broadcasted_iota(jnp.int32, (40, LANES), 1)
    source[last : last + 40] = jnp.where(lane < edge, tail[7:47], tail[8:48])

    def align(step, carry):
        at = pl.multiple_of(step * 80, 8)
        flat[pl.ds(at, 80), :] = shifted_rows(source, start, shift, at, 80)
        return carry

    lax.fori_loop(0, SHIFT_ROWS // 80, align, 0)

    def rows(first, count, stride):
        return flat[pl.ds(first, count, stride), :]

    def plain(base, count, to):
        for m in range(8):
            tile = rows(base + m, count, 8)
            a, b = tile[: count // 2], tile[count // 2 :]
            out[2 * m, to : to + count // 2] = join(a, 0, b, 0).astype(BF16)
            out[2 * m + 1, to : to + count // 2] = join(a, 1, b, 1).astype(BF16)

    def expand(base, count, to):
        for r in range(16):
            out[r, to : to + count] = rows(base + 2 * r, count, 32).astype(BF16)
            out[r, to + count : to + 2 * count] = rows(base + 2 * r + 1, count, 32).astype(BF16)

    def project(base):
        for m in range(8):
            first, middle, last = (rows(base + 3 * m + j, 128, 24) for j in range(3))
            out[2 * m, 0:128] = first.astype(BF16)
            out[2 * m, 128:192] = join(middle[:64], 0, middle[64:], 0).astype(BF16)
            out[2 * m + 1, 0:128] = join(middle, 1, last, 0).astype(BF16)
            out[2 * m + 1, 128:192] = join(last[:64], 1, last[64:], 1).astype(BF16)

    @pl.when(kind == PROJECT)
    def _():
        project(LEAD)

    @pl.when(kind == PLAIN)
    def _():
        plain(LEAD, 384, 0)

    @pl.when(kind == PLAIN_EXPAND)
    def _():
        plain(LEAD, 256, 0)
        expand(LEAD + 2048 + 8, 32, 128)

    @pl.when(kind == EXPAND)
    def _():
        expand(LEAD, 96, 0)

    @pl.when(kind == EXPAND_PLAIN)
    def _():
        expand(LEAD, 32, 0)
        plain(LEAD + 1024 + 32, 256, 64)

    vectors = flat[pl.ds(vector_row, 32), :].astype(BF16)
    for r in range(16):
        out[r, PIECE : PIECE + 32] = vectors
        out[r, PIECE + 32 :] = places[...]


def spread(source, at, vectors, to):
    tile = source[pl.ds(at, 8), :].astype(F32)
    for j in range(8):
        vectors[to : to + 1, 128 * j : 128 * j + 128] = tile[j : j + 1]


def project_in_body(scalars, own, came, qkv_w, vectors, qkv_b, project_rows):
    head = scalars[0]
    low = low_lanes((64, LANES))
    vectors[...] = jnp.zeros(vectors.shape, F32)

    def take(got):
        for c in range(8):
            qkv_w[128 * c : 128 * c + 128, 0:128] = got[c, 0:128]
            packed = got[c, 128:192].astype(F32)
            qkv_w[128 * c : 128 * c + 64, 128:256] = jnp.where(low, packed, 0.0).astype(BF16)
            qkv_w[128 * c + 64 : 128 * c + 128, 128:256] = jnp.where(low, swap(packed), 0.0).astype(BF16)
        project_rows[0:32] = got[0, PIECE : PIECE + 32].astype(F32)
        for v in range(4):
            spread(project_rows, 8 * v, vectors, v)
        project_rows[0:24] = got[8, PIECE + 8 : PIECE + 32].astype(F32)

    pl.when(scalars[1] == 0)(lambda: take(own))
    pl.when(scalars[1] != 0)(lambda: take(came))
    row = head // 2 * 3
    first, middle, last = (project_rows[pl.ds(row + j, 1), :] for j in range(3))
    odd = head % 2 == 1
    qkv_b[0:1, 0:128] = jnp.where(odd, join(middle, 1, last, 0), first)
    value = jnp.where(odd, swap(last), middle)
    qkv_b[0:1, 128:256] = jnp.where(low_lanes((1, LANES)), value, 0.0)


def rest_in_body(scalars, own, came, expand_w, second, biases, expand_b, rows):
    head = scalars[0]
    biases[...] = jnp.zeros(biases.shape, F32)

    def take(lower, upper):
        def block(c, at, count):
            return (lower if c < 16 else upper)[c % 16, at : at + count]

        for c, at, row, count in expand_places():
            expand_w[row : row + count, 0:128] = block(c, at, count)
            expand_w[row : row + count, 128:256] = block(c, at + count, count)

        def tile(place):
            c, at, row, half = place
            return block(c, at + row, 64).astype(F32), half

        for h in range(16):
            a, half = tile(dense_place(64 * h))
            second[h, 0:32] = join(a[:32], half, a[32:], half).astype(BF16)
            for part in range(2):
                a, half = tile(shrink_place(256 * h + 64 * part))
                b, other = tile(shrink_place(256 * h + 128 + 64 * part))
                second[h, 32 + 64 * part : 96 + 64 * part] = join(a, half, b, other).astype(BF16)
        for to, c in enumerate((10, 31)):
            rows[0:16] = block(c, PIECE, 16).astype(F32)
            spread(rows, 0, biases, to)
        rows[...] = block(21, PIECE, 32).astype(F32)

    pl.when(scalars[1] == 0)(lambda: take(own, came))
    pl.when(scalars[1] != 0)(lambda: take(came, own))
    expand_b[0:1, 0:128] = rows[pl.ds(2 * head, 1), :]
    expand_b[0:1, 128:256] = rows[pl.ds(2 * head + 1, 1), :]


def rows_in_body(got, dense_w, shrink_w):
    for m in range(8):
        even, odd = got[2 * m].astype(F32), got[2 * m + 1].astype(F32)
        columns = slice(128 * m, 128 * m + 128)
        for out, at, half in ((dense_w, 0, 32), (shrink_w, 32, 128)):
            a, b = even[at : at + half], odd[at : at + half]
            out[0:half, columns] = join(a, 0, b, 0).astype(BF16)
            out[half : 2 * half, columns] = join(a, 1, b, 1).astype(BF16)


def rows_out_body(dense_g, shrink_g, out):
    for m in range(8):
        columns = slice(128 * m, 128 * m + 128)
        for source, at, half in ((dense_g, 0, 32), (shrink_g, 32, 128)):
            a, b = source[0:half, columns], source[half : 2 * half, columns]
            out[2 * m, at : at + half] = join(a, 0, b, 0).astype(BF16)
            out[2 * m + 1, at : at + half] = join(a, 1, b, 1).astype(BF16)


def early_body(scalars, second, expand_g, bias_g, expand_bg, own, other, expand_rows):
    head = scalars[0]
    expand_rows[...] = jnp.zeros(expand_rows.shape, F32)
    expand_rows[pl.ds(2 * head, 1), :] = expand_bg[0:1, 0:128]
    expand_rows[pl.ds(2 * head + 1, 1), :] = expand_bg[0:1, 128:256]
    rows = [bias_g[0:1, 128 * j : 128 * j + 128] for j in range(8)]
    bias = jnp.concatenate(rows + [jnp.zeros((8, LANES), F32)], axis=0).astype(BF16)

    def dense_rows(row):
        packed = second[row // 64, 0:32].astype(F32)
        return jnp.concatenate([packed, swap(packed)], axis=0)

    def shrink_rows(row):
        h, part = row // 256, row % 256 // 64
        packed = second[h, 32 + part % 2 * 64 : 96 + part % 2 * 64].astype(F32)
        return swap(packed) if part >= 2 else packed

    def put(lower, upper):
        def store(c, at, tile):
            (lower if c < 16 else upper)[c % 16, at : at + tile.shape[0]] = tile

        def plain(c, to, base, count, take):
            for i in range(count // 128):
                a, b = take(base + 64 * i), take(base + count // 2 + 64 * i)
                store(c, to + 64 * i, join(a, 0, b, 0).astype(BF16))

        for c in range(8):
            store(c, 0, jnp.zeros((PIECE, LANES), BF16))
        for c in range(OWNERS):
            store(c, PIECE, jnp.zeros((32, LANES), BF16))
        for c, at, row, count in expand_places():
            store(c, at, expand_g[row : row + count, 0:128].astype(BF16))
            store(c, at + count, expand_g[row : row + count, 128:256].astype(BF16))
        plain(8, 0, 0, 384, dense_rows)
        plain(9, 0, 384, 384, dense_rows)
        plain(10, 0, 768, 256, dense_rows)
        plain(21, 64, 0, 256, shrink_rows)
        for c in range(22, 32):
            plain(c, 0, 256 + 384 * (c - 22), 384, shrink_rows)
        store(10, PIECE, bias)
        store(31, PIECE, bias)
        store(21, PIECE, expand_rows[...].astype(BF16))

    pl.when(scalars[1] == 0)(lambda: put(own, other))
    pl.when(scalars[1] != 0)(lambda: put(other, own))


LATE_ROWS = 8 * PIECE + 64


def late_body(scalars, qkv_g, vector_g, qkv_bg, out, project_rows):
    head = scalars[0]
    for c in range(8):
        at = PIECE * c
        out[at : at + 128] = qkv_g[128 * c : 128 * c + 128, 0:128].astype(BF16)
        a = qkv_g[128 * c : 128 * c + 64, 128:256]
        b = qkv_g[128 * c + 64 : 128 * c + 128, 128:256]
        out[at + 128 : at + 192] = join(a, 0, b, 0).astype(BF16)
    gains = [vector_g[v : v + 1, 128 * j : 128 * j + 128] for v in range(4) for j in range(8)]
    out[8 * PIECE : 8 * PIECE + 32] = jnp.concatenate(gains, axis=0).astype(BF16)
    project_rows[...] = jnp.zeros(project_rows.shape, F32)
    pair, value = qkv_bg[0:1, 0:128], qkv_bg[0:1, 128:256]
    low = low_lanes((1, LANES))
    row = 8 + head // 2 * 3
    odd = head % 2 == 1
    project_rows[pl.ds(row, 1), :] = jnp.where(odd, 0.0, pair)
    project_rows[pl.ds(row + 1, 1), :] = jnp.where(
        odd, jnp.where(low, 0.0, swap(pair)), jnp.where(low, value, 0.0)
    )
    project_rows[pl.ds(row + 2, 1), :] = jnp.where(odd, join(pair, 1, value, 0), 0.0)
    out[8 * PIECE + 32 :] = project_rows[...].astype(BF16)


def both_body(scalars, early, early_came, late, late_came, out):
    def add(r, carry):
        out[r] = (early[r].astype(F32) + early_came[r].astype(F32)).astype(BF16)
        return carry

    lax.fori_loop(0, 16, add, 0)

    @pl.when(scalars[0] == 0)
    def _():
        def total(at, count):
            return (late[at : at + count].astype(F32) + late_came[at : at + count].astype(F32)).astype(BF16)

        for c in range(8):
            out[c, 0:PIECE] = total(PIECE * c, PIECE)
        out[0, PIECE : PIECE + 32] = total(8 * PIECE, 32)
        out[8, PIECE : PIECE + 32] = total(8 * PIECE + 32, 32)


BACK_ROWS = PIECE + 32
TAKE_ROWS = 3120


def grads_in_body(scalars, got, out, flat):
    start, shift, kind, vector_row = scalars[0], scalars[1], scalars[2], scalars[3]
    lead = LEAD + 8

    def clear(step, carry):
        flat[pl.ds(pl.multiple_of(step * 80, 8), 80), :] = jnp.zeros((80, LANES), F32)
        return carry

    lax.fori_loop(0, SHIFT_ROWS // 80, clear, 0)

    def add_vectors(source, total):
        return total + got[source, PIECE : PIECE + 32].astype(F32)

    flat[pl.ds(vector_row + 8, 32), :] = lax.fori_loop(0, 16, add_vectors, jnp.zeros((32, LANES), F32))

    def taken(r, at, count):
        return got[r, at : at + count].astype(F32)

    def plain(base, count, at):
        half = count // 2
        for m in range(8):
            a, b = taken(2 * m, at, half), taken(2 * m + 1, at, half)
            flat[pl.ds(base + m, half, 8), :] = join(a, 0, b, 0)
            flat[pl.ds(base + m + 8 * half, half, 8), :] = join(a, 1, b, 1)

    def expand(base, count, at):
        for r in range(16):
            flat[pl.ds(base + 2 * r, count, 32), :] = taken(r, at, count)
            flat[pl.ds(base + 2 * r + 1, count, 32), :] = taken(r, at + count, count)

    def project(base):
        for m in range(8):
            pair, values = taken(2 * m, 0, 128), taken(2 * m, 128, 64)
            odd_pair, odd_values = taken(2 * m + 1, 0, 128), taken(2 * m + 1, 128, 64)
            values = jnp.concatenate([values, swap(values)], axis=0)
            odd_values = jnp.concatenate([odd_values, swap(odd_values)], axis=0)
            flat[pl.ds(base + 3 * m, 128, 24), :] = pair
            flat[pl.ds(base + 3 * m + 1, 128, 24), :] = join(values, 0, odd_pair, 0)
            flat[pl.ds(base + 3 * m + 2, 128, 24), :] = join(odd_pair, 1, odd_values, 0)

    @pl.when(kind == PROJECT)
    def _():
        project(lead)

    @pl.when(kind == PLAIN)
    def _():
        plain(lead, 384, 0)

    @pl.when(kind == PLAIN_EXPAND)
    def _():
        plain(lead, 256, 0)
        expand(lead + 2048 + 8, 32, 128)

    @pl.when(kind == EXPAND)
    def _():
        expand(lead, 96, 0)

    @pl.when(kind == EXPAND_PLAIN)
    def _():
        expand(lead, 32, 0)
        plain(lead + 1024 + 32, 256, 64)

    def align(step, carry):
        at = pl.multiple_of(step * 80, 8)
        out[pl.ds(at, 80), :] = shifted_rows(flat, start, shift, at, 80)
        return carry

    lax.fori_loop(0, TAKE_ROWS // 80, align, 0)


def token_rows(ref):
    return jnp.concatenate([ref[0, 0, 0], ref[1, 0, 0], ref[0, 0, 1], ref[1, 0, 1]], axis=0)


def put_rows(kept, sent, rows, core):
    step = rows.shape[0] // 4
    for x in range(2):
        first, second = (rows[step * i : step * i + step].astype(BF16) for i in (2 * x, 2 * x + 1))
        kept[0, x] = jnp.where(core == 0, first, second)
        sent[0, x] = jnp.where(core == 0, second, first)


def relative_place(i, here):
    y = (i & 1) ^ here[2]
    z = (i >> 1) ^ here[3]
    return y * 4 + (z & 1) * 2 + (z >> 1)


def normalized(values):
    centered = values - jnp.mean(values, axis=-1, keepdims=True)
    variance = jnp.mean(centered * centered, axis=-1, keepdims=True)
    return centered * lax.rsqrt(variance + EPSILON)


def turned(pair, cos, sin):
    lane = lax.broadcasted_iota(jnp.int32, pair.shape, 1) % HD
    half = ROT // 2
    other = jnp.where(
        lane < half, -pltpu.roll(pair, LANES - half, 1), jnp.where(lane < ROT, pltpu.roll(pair, half, 1), 0.0)
    )
    return pair * cos + other * sin


def mixed_body(tokens, place, vectors, qkv_w, qkv_b, inverse, one, two, query, key, value, cos, sin):
    unit = normalized(token_rows(tokens).astype(F32))
    angles = place[...] * inverse[...]
    cos[...] = jnp.cos(angles)
    sin[...] = jnp.sin(angles)
    first = (unit * vectors[0:1] + vectors[1:2]).astype(BF16)
    one[...] = first
    two[...] = (unit * vectors[2:3] + vectors[3:4]).astype(BF16)
    mixed = mm(first, qkv_w[...]) + qkv_b[...]
    pair = turned(mixed[:, :LANES], cos[...], sin[...])
    query[...] = pair[:, :HD].astype(BF16) * HD ** (-0.5)
    key[...] = pair[:, HD:].astype(BF16)
    value[...] = mixed[:, LANES : LANES + HD].astype(BF16)


def masked_scores(key, query_t, at, first_query, length):
    scores = mm(key, query_t)
    keys = at * BLOCK + lax.broadcasted_iota(jnp.int32, scores.shape, 0)
    queries = first_query + lax.broadcasted_iota(jnp.int32, scores.shape, 1)
    return jnp.where((keys <= queries) & (keys < length), scores, NEGATIVE)


def folded(values, op):
    parts = [values[8 * i : 8 * i + 8] for i in range(values.shape[0] // 8)]
    while len(parts) > 1:
        parts = [op(a, b) for a, b in zip(parts[::2], parts[1::2])]
    return parts[0]


def attend_body(lengths, query, key, value, low_out, full_out, log_out, scores, value_t):
    at = pl.program_id(0)
    length = lengths[0]

    @pl.when(at == 0)
    def _():
        value_t[...] = value[...].astype(F32).T.astype(BF16)

    query_t = query[...].astype(F32).T.astype(BF16)
    clear = jnp.minimum(at, length // BLOCK)
    stop = jnp.minimum(at, (length - 1) // BLOCK) + 1

    def rows(j):
        return pl.ds(pl.multiple_of(j * BLOCK, BLOCK), BLOCK)

    def score(j, top, masked):
        if masked:
            tile = masked_scores(key[rows(j), :], query_t, j, at * BLOCK, length)
        else:
            tile = mm(key[rows(j), :], query_t)
        scores[rows(j), :] = tile
        return jnp.maximum(top, folded(tile, jnp.maximum))

    top = jnp.full((8, BLOCK), NEGATIVE, F32)
    top = lax.fori_loop(0, clear, lambda j, t: score(j, t, False), top)
    top = lax.fori_loop(clear, stop, lambda j, t: score(j, t, True), top)
    top = jnp.max(top, axis=0, keepdims=True)

    def weigh(j, carried):
        total, out = carried
        tile = jnp.exp(scores[rows(j), :] - top)
        return total + folded(tile, jnp.add), out + mm(value_t[:, rows(j)], tile.astype(BF16))

    start = (jnp.zeros((8, BLOCK), F32), jnp.zeros((HD, BLOCK), F32))
    total, out = lax.fori_loop(0, stop, weigh, start)
    total = jnp.sum(total, axis=0, keepdims=True)
    out = out * (1.0 / total)
    full_out[...] = out
    low_out[...] = out.T.astype(BF16)
    log_out[...] = top + jnp.log(total)


def attend_back_body(
    lengths, query, key, value, grad, full_out, log_in, query_g, key_g, value_g, key_t, key_sum, value_sum
):
    at = pl.program_id(0)
    length = lengths[0]

    @pl.when(at == 0)
    def _():
        key_t[...] = key[...].astype(F32).T.astype(BF16)
        key_sum[...] = jnp.zeros(key_sum.shape, F32)
        value_sum[...] = jnp.zeros(value_sum.shape, F32)

    query_rows, grad_rows = query[...], grad[...]
    query_t = query_rows.astype(F32).T.astype(BF16)
    grad_full_t = grad_rows.astype(F32).T
    grad_t = grad_full_t.astype(BF16)
    delta = jnp.sum(grad_full_t * full_out[...], axis=0, keepdims=True)
    log_total = log_in[...]
    clear = jnp.minimum(at, length // BLOCK)
    stop = jnp.minimum(at, (length - 1) // BLOCK) + 1
    clear, stop = (jnp.where(at * BLOCK < length, n, 0) for n in (clear, stop))

    def step(j, query_sum, masked):
        rows = pl.ds(pl.multiple_of(j * BLOCK, BLOCK), BLOCK)
        if masked:
            tile = masked_scores(key[rows, :], query_t, j, at * BLOCK, length)
        else:
            tile = mm(key[rows, :], query_t)
        probs = jnp.exp(tile - log_total)
        value_sum[rows, :] += mm(probs.astype(BF16), grad_rows)
        score_g = (probs * (mm(value[rows, :], grad_t) - delta)).astype(BF16)
        key_sum[rows, :] += mm(score_g, query_rows)
        return query_sum + mm(key_t[:, rows], score_g)

    query_sum = jnp.zeros((HD, BLOCK), F32)
    query_sum = lax.fori_loop(0, clear, lambda j, s: step(j, s, False), query_sum)
    query_sum = lax.fori_loop(clear, stop, lambda j, s: step(j, s, True), query_sum)
    query_g[...] = (query_sum * HD ** (-0.5)).T.astype(BF16)

    @pl.when(at == pl.num_programs(0) - 1)
    def _():
        key_g[...] = key_sum[...].astype(BF16)
        value_g[...] = value_sum[...].astype(BF16)


def feed_body(
    here, two, attended, cotangent, expand_w, expand_b, shrink_w, dense_w,
    partial_out, attended_g, hidden_g, shrink_g, dense_g, expand_g, expand_bg, bias_g,
):
    at = pl.program_id(0)

    @pl.when(at == 0)
    def _():
        for total in (shrink_g, dense_g, expand_g, expand_bg, bias_g):
            total[...] = jnp.zeros(total.shape, F32)

    normed, mixed = two[...], attended[...]
    hidden = mm(normed, expand_w[...]) + expand_b[...]
    error = lax.erf(hidden * math.sqrt(0.5))
    cumulative = 0.5 * (1.0 + error)
    active = (hidden * cumulative).astype(BF16)
    partial = mm(mixed, dense_w[...]) + mm(active, shrink_w[...])
    step = BLOCK // 4
    for i, (core, x) in enumerate(((0, 0), (1, 0), (0, 1), (1, 1))):
        partial_out[core, 0, x] = partial[step * i : step * i + step].astype(BF16)
    token = at * BLOCK + lax.broadcasted_iota(jnp.int32, (BLOCK, D), 0)
    seed = jnp.where(token < here[0], token_rows(cotangent).astype(F32), 0.0)
    bias_g[...] += jnp.sum(seed, axis=0, keepdims=True)
    seed = seed.astype(BF16)
    attended_g[...] = mm(seed, dense_w[...], ((1,), (1,))).astype(BF16)
    slope = cumulative + hidden * jnp.exp(-0.5 * hidden * hidden) * (1.0 / math.sqrt(2.0 * math.pi))
    back = (mm(seed, shrink_w[...], ((1,), (1,))) * slope).astype(BF16)
    hidden_g[...] = back
    expand_bg[...] += jnp.sum(back.astype(F32), axis=0, keepdims=True)
    shrink_g[...] += mm(active, seed, ((0,), (0,)))
    dense_g[...] += mm(mixed, seed, ((0,), (0,)))
    expand_g[...] += mm(normed, back, ((0,), (0,)))


def mixed_back_body(
    here, tokens, one, query_g, key_g, value_g, hidden_g, vectors, qkv_w, expand_w, cos, sin,
    kept, sent, qkv_g, qkv_bg, vector_g,
):
    at = pl.program_id(0)

    @pl.when(at == 0)
    def _():
        for total in (qkv_g, qkv_bg, vector_g):
            total[...] = jnp.zeros(total.shape, F32)

    pair = jnp.concatenate([query_g[...].astype(F32), key_g[...].astype(F32)], axis=1)
    pair = turned(pair, cos[...], -sin[...])
    values = value_g[...].astype(F32)
    mixed_g = jnp.concatenate([pair, values, jnp.zeros_like(values)], axis=1)
    mixed_low = mixed_g.astype(BF16)
    qkv_bg[...] += jnp.sum(mixed_low.astype(F32), axis=0, keepdims=True)
    qkv_g[...] += mm(one[...], mixed_low, ((0,), (0,)))
    one_g = mm(mixed_low, qkv_w[...], ((1,), (1,)))
    two_g = mm(hidden_g[...], expand_w[...], ((1,), (1,)))
    unit = normalized(token_rows(tokens).astype(F32))
    vector_g[0:1] += jnp.sum(one_g * unit, axis=0, keepdims=True)
    vector_g[1:2] += jnp.sum(one_g, axis=0, keepdims=True)
    vector_g[2:3] += jnp.sum(two_g * unit, axis=0, keepdims=True)
    vector_g[3:4] += jnp.sum(two_g, axis=0, keepdims=True)
    put_rows(kept, sent, one_g * vectors[0:1] + two_g * vectors[2:3], here[1])


def split_mesh(mesh):
    groups, members = mesh.shape["blk"], mesh.shape["uly"]
    return Mesh(mesh.devices.reshape(groups // 2, 2, members // 2, 2), ALL)


def across_x(block):
    return lax.ppermute(block, "x", [(0, 1), (1, 0)])


def by_head(residual, cotangent, lengths, positions, masters, momenta, averages):
    slots, span, width = residual.shape
    x = lax.axis_index("x")
    head = lax.axis_index("core") * 8 + lax.axis_index("z") * 2 + lax.axis_index("y")
    owner = x * 16 + head
    groups = lax.axis_size("z") * lax.axis_size("y")
    count = groups * 4 * span
    chunk = masters.shape[0]
    length = lax.dynamic_slice_in_dim(lengths, x, 1)

    def paired(mine, theirs):
        return jnp.where(x == 0, jnp.stack([mine, theirs]), jnp.stack([theirs, mine]))

    def at_x(rows, index):
        return lax.dynamic_index_in_dim(rows, index, 0, keepdims=False)

    rows = jnp.stack([residual, cotangent], axis=1)
    rows = paired(at_x(rows, x), across_x(at_x(rows, 1 - x)))
    places = paired(at_x(positions, x), across_x(at_x(positions, 1 - x))).reshape(1, 2 * span)
    tokens_shape = (2, groups, 2, span, width)
    slot_tokens = lax.all_gather(rows[:, 0], RING, axis=0).reshape(tokens_shape)
    slot_cotangent = lax.all_gather(rows[:, 1], RING, axis=0).reshape(tokens_shape)
    high, rest = (places // 256).astype(BF16), (places % 256).astype(BF16)
    places = jnp.concatenate([high, rest, jnp.zeros((14, 2 * span), BF16)])
    lane = jnp.arange(LANES, dtype=jnp.int32) % HD
    inverse = ROTARY_BASE ** (-((lane % (ROT // 2)).astype(F32) * 2.0 / ROT))
    inverse = jnp.where(lane < ROT, inverse, 0.0)[None, :]

    onward = [(i, i + 1) for i in range(OWNERS - 1)]
    backward = [(i + 1, i) for i in range(OWNERS - 1)]
    before = lax.ppermute(masters[chunk - D :], ALL, onward)
    after = lax.ppermute(masters[: 4 * D], ALL, backward)
    own_rows = -(-chunk // D) * 8
    own = jnp.pad(masters, (0, own_rows * LANES - chunk)).reshape(own_rows, LANES)
    before, after = before.reshape(8, LANES), after.reshape(32, LANES)
    skipped = jnp.where(owner < 8, 4, jnp.where(owner < 11, 7, jnp.where(owner < 22, 8, 12)))
    kind = jnp.where(
        owner < 8,
        PROJECT,
        jnp.where(
            owner == 10,
            PLAIN_EXPAND,
            jnp.where(owner == 21, EXPAND_PLAIN, jnp.where((owner > 10) & (owner < 21), EXPAND, PLAIN)),
        ),
    )
    vector_row = jnp.where(owner == 10, 2080, jnp.where(owner == 21, 1056, jnp.where(owner == 31, 3104, 0)))
    ahead = skipped * D - (chunk - PER * D) * owner
    begin = ahead + 4 * D
    scalars = jnp.stack([begin // LANES, begin % LANES, kind, vector_row]).astype(jnp.int32)
    sent = call(
        weights_out_body, (1,),
        [whole(before.shape), whole(own.shape), whole(after.shape), whole(places.shape)],
        whole((16, SEND_ROWS, LANES)),
        shaped((16, SEND_ROWS, LANES), BF16),
        [pltpu.VMEM((3280, LANES), F32), pltpu.VMEM((SHIFT_ROWS, LANES), F32), pltpu.VMEM((48, LANES), F32)],
        1,
    )(scalars, before, own, after, places)
    got = lax.all_to_all(sent, RING, 0, 0, tiled=True)
    head_scalar = jnp.stack([head, x]).astype(jnp.int32)
    place = got[:, PIECE + 32 : PIECE + 34].astype(F32).reshape(2, groups, 2, 2, span)
    place = (place[:, :, 0] * 256.0 + place[:, :, 1]).transpose(1, 2, 0, 3).reshape(count, 1)
    came = lax.ppermute(got[:9], "x", [(0, 1)])
    qkv_w, vectors, qkv_b = call(
        project_in_body, (1,),
        [whole((9, SEND_ROWS, LANES)), whole((9, SEND_ROWS, LANES))],
        [whole((D, 256)), whole((8, D)), whole((1, 256))],
        [shaped((D, 256), BF16), shaped((8, D), F32), shaped((1, 256), F32)],
        [pltpu.VMEM((32, LANES), F32)], 1,
    )(head_scalar, got, came)
    came = across_x(got)
    expand_w, second, biases, expand_b = call(
        rest_in_body, (1,),
        [whole(got.shape), whole(got.shape)],
        [whole((D, 256)), whole((16, 160, LANES)), whole((8, D)), whole((1, 256))],
        [shaped((D, 256), BF16), shaped((16, 160, LANES), BF16), shaped((8, D), F32), shaped((1, 256), F32)],
        [pltpu.VMEM((32, LANES), F32)], 1,
    )(head_scalar, got, came)
    second = lax.all_to_all(second, RING, 0, 0, tiled=True)
    steps = (count // BLOCK,)
    token_spec = pl.BlockSpec((2, 1, 2, span, width), lambda i, *_: (0, i, 0, 0, 0))
    part_spec = pl.BlockSpec((1, 2, span, width), lambda i, here: (relative_place(i, here), 0, 0, 0))
    part_shape = shaped((groups, 2, span, width), BF16)
    y, z, core = lax.axis_index("y"), lax.axis_index("z"), lax.axis_index("core")
    here = jnp.stack([length[0], core, y, z]).astype(jnp.int32)

    swap_pair, far_pairs = [(0, 1), (1, 0)], [(0, 2), (2, 0), (1, 3), (3, 1)]

    def summed(kept, sent):
        left = kept.shape[0]
        for axis, route in (
            ("core", swap_pair), ("y", swap_pair), ("z", swap_pair + [(2, 3), (3, 2)]), ("z", far_pairs)
        ):
            came = lax.ppermute(sent, axis, route)
            if left == 1:
                return (kept[0].astype(F32) + came[0].astype(F32)).astype(BF16)
            left //= 2
            kept, sent = [
                (kept[half].astype(F32) + came[half].astype(F32)).astype(BF16)
                for half in (slice(0, left), slice(left, None))
            ]

    def to_owner(rows):
        mine, theirs = at_x(rows, x), at_x(rows, 1 - x)
        return paired(mine, across_x(theirs)).astype(F32)

    def rows_spec(columns):
        return pl.BlockSpec((BLOCK, columns), lambda i, *_: (i, 0))

    def columns_spec(rows):
        return pl.BlockSpec((rows, BLOCK), lambda i, *_: (0, i))

    narrow = shaped((count, HD), BF16)
    table = shaped((count, LANES), F32)
    one, two, query, key, value, cos, sin = call(
        mixed_body, steps,
        [token_spec, rows_spec(1), whole((8, D)), whole((D, 256)), whole((1, 256)), whole((1, LANES))],
        [rows_spec(D), rows_spec(D), rows_spec(HD), rows_spec(HD), rows_spec(HD), rows_spec(LANES), rows_spec(LANES)],
        [shaped((count, D), BF16), shaped((count, D), BF16), narrow, narrow, narrow, table, table],
    )(slot_tokens, place, vectors, qkv_w, qkv_b, inverse)
    attended, attended_full, log_total = call(
        attend_body, steps,
        [rows_spec(HD), whole((count, HD)), whole((count, HD))],
        [rows_spec(HD), columns_spec(HD), columns_spec(1)],
        [narrow, shaped((HD, count), F32), shaped((1, count), F32)],
        [pltpu.VMEM((count, BLOCK), F32), pltpu.VMEM((HD, count), BF16)], 1,
    )(length, query, key, value)
    second, attended = lax.optimization_barrier((second, attended))
    dense_w, shrink_w = call(
        rows_in_body, (1,), [whole(second.shape)], [whole((HD, D)), whole((256, D))],
        [shaped((HD, D), BF16), shaped((256, D), BF16)],
    )(second)

    partial_out, attended_g, hidden_g, shrink_g, dense_g, expand_g, expand_bg, bias_g = call(
        feed_body, steps,
        [rows_spec(D), rows_spec(HD), token_spec, whole((D, 256)), whole((1, 256)), whole((256, D)), whole((HD, D))],
        [token_spec, rows_spec(HD), rows_spec(256), whole((256, D)), whole((HD, D)), whole((D, 256)),
         whole((1, 256)), whole((1, D))],
        [shaped(tokens_shape, BF16), narrow, shaped((count, 256), BF16), shaped((256, D), F32), shaped((HD, D), F32),
         shaped((D, 256), F32), shaped((1, 256), F32), shaped((1, D), F32)], (), 1,
    )(here, two, attended, slot_cotangent, expand_w, expand_b, shrink_w, dense_w)
    second_g = call(
        rows_out_body, (1,), [whole((HD, D)), whole((256, D))], whole((16, 160, LANES)),
        shaped((16, 160, LANES), BF16),
    )(dense_g, shrink_g)
    attended_g, second_g = lax.optimization_barrier((attended_g, second_g))
    second_g = lax.all_to_all(second_g, RING, 0, 0, tiled=True)
    out_rows = lax.psum_scatter(
        partial_out.reshape(16, 2, span, width), RING, scatter_dimension=0, tiled=True
    )[0]
    out_rows = to_owner(out_rows)
    query_g, key_g, value_g = call(
        attend_back_body, steps,
        [rows_spec(HD), whole((count, HD)), whole((count, HD)), rows_spec(HD), columns_spec(HD), columns_spec(1)],
        [rows_spec(HD), whole((count, HD)), whole((count, HD))],
        [narrow, narrow, narrow],
        [pltpu.VMEM((HD, count), BF16), pltpu.VMEM((count, HD), F32), pltpu.VMEM((count, HD), F32)],
        1,
    )(length, query, key, value, attended_g, attended_full, log_total)
    bias_g = jnp.where(head == 0, bias_g, 0.0)
    plane = (16, BACK_ROWS, LANES)
    early, early_other = call(
        early_body, (1,),
        [whole((16, 160, LANES)), whole((D, 256)), whole((1, D)), whole((1, 256))],
        [whole(plane), whole(plane)],
        [shaped(plane, BF16), shaped(plane, BF16)],
        [pltpu.VMEM((32, LANES), F32)], 1,
    )(head_scalar, second_g, expand_g, bias_g, expand_bg)
    early_came = across_x(early_other)
    kept, sent, qkv_g, qkv_bg, vector_g = call(
        mixed_back_body, steps,
        [token_spec, rows_spec(D), rows_spec(HD), rows_spec(HD), rows_spec(HD),
         rows_spec(256), whole((8, D)), whole((D, 256)), whole((D, 256)), rows_spec(LANES), rows_spec(LANES)],
        [part_spec, part_spec, whole((D, 256)), whole((1, 256)), whole((8, D))],
        [part_shape, part_shape, shaped((D, 256), F32), shaped((1, 256), F32), shaped((8, D), F32)], (), 1,
    )(here, slot_tokens, one, query_g, key_g, value_g, hidden_g, vectors, qkv_w, expand_w, cos, sin)
    in_rows = to_owner(summed(kept, sent))

    values = residual.astype(F32)
    middle = jnp.mean(values, axis=-1, keepdims=True)
    scale = lax.rsqrt(jnp.mean((values - middle) ** 2, axis=-1, keepdims=True) + EPSILON)
    middle, scale = lax.optimization_barrier((middle, scale))

    late = call(
        late_body, (1,), [whole((D, 256)), whole((8, D)), whole((1, 256))], whole((LATE_ROWS, LANES)),
        shaped((LATE_ROWS, LANES), BF16), [pltpu.VMEM((32, LANES), F32)], 1,
    )(head_scalar, qkv_g, vector_g, qkv_bg)
    late_came = lax.ppermute(late, "x", [(1, 0)])
    x_scalar = x.astype(jnp.int32).reshape(1)
    sent_g = call(
        both_body, (1,),
        [whole(plane), whole(plane), whole((LATE_ROWS, LANES)), whole((LATE_ROWS, LANES))],
        whole(plane), shaped(plane, BF16), (), 1,
    )(x_scalar, early, early_came, late, late_came)
    got_g = lax.all_to_all(sent_g, RING, 0, 0, tiled=True)
    begin_g = (chunk - PER * D) * owner - skipped * D + 4 * D
    scalars_g = jnp.stack([begin_g // LANES, begin_g % LANES, kind, vector_row]).astype(jnp.int32)
    taken = call(
        grads_in_body, (1,), [whole(got_g.shape)], whole((TAKE_ROWS, LANES)), shaped((TAKE_ROWS, LANES), F32),
        [pltpu.VMEM((SHIFT_ROWS, LANES), F32)], 1,
    )(scalars_g, got_g).reshape(-1)
    from_before = lax.ppermute(taken[D + chunk : 5 * D + chunk], ALL, onward)
    from_after = lax.ppermute(taken[:D], ALL, backward)
    gradients = (
        taken[D : D + chunk]
        + jnp.pad(from_before, (0, chunk - 4 * D))
        + jnp.pad(from_after, (chunk - D, 0))
    )

    outputs = (values + out_rows + (biases[0] + biases[1])).astype(BF16)
    first_token = ((lax.axis_index("z") * 2 + lax.axis_index("y")) * 4 + x * 2 + lax.axis_index("core")) * span
    token = first_token + jnp.arange(span, dtype=jnp.int32)
    live = token[None, :] < lengths[:, None]
    seed = jnp.where(live[:, :, None], cotangent.astype(F32), 0.0)
    unit = (values - middle) * scale
    back = in_rows - jnp.mean(in_rows, axis=-1, keepdims=True)
    back = scale * (back - unit * jnp.mean(in_rows * unit, axis=-1, keepdims=True))
    input_grad = (seed + back).astype(BF16)

    velocity = MOMENTUM * momenta + gradients
    step_rate = LEARN_RATE / math.sqrt(slots * count)
    updated = masters - step_rate * (gradients + MOMENTUM * velocity)
    averaged = AVERAGE_DECAY * averages + (1.0 - AVERAGE_DECAY) * updated
    return (outputs, input_grad, gradients, updated, velocity, averaged)


def solution(mesh):
    fits = mesh.size == OWNERS and mesh.shape["blk"] == 4

    def step(*args):
        slots, tokens = args[0].shape[:2]
        if fits and slots * H == OWNERS and tokens == 64 * OWNERS:
            tokens_in, flat, used, body = P(None, ("z", "y", "x", "core"), None), P(ALL), split_mesh(mesh), by_head
            places = P(None, ("z", "y", "x", "core"))
        else:
            tokens_in, flat, used, body = P(None, ("uly", "blk"), None), P(("blk", "uly")), mesh, local
            places = P(None, ("uly", "blk"))
        return jax.shard_map(
            body,
            mesh=used,
            in_specs=(tokens_in, tokens_in, P(), places, flat, flat, flat),
            out_specs=(tokens_in, tokens_in, flat, flat, flat, flat),
            check_vma=False,
        )(*args)

    return step
```

profile of v0, /device:TPU:0, one launch (start us, length us, event | category | flops | bytes accessed | tf_op | source)
XLA Modules:
  0.0 411.2 jit_solution(7057913471372529182)
XLA Ops:
  11.4 6.3 %collective-permute-done = bf16[2,64,1024]{2,1,0:T(8,128)(2,1)S(1)} collective-permute-done((bf16[2,64,1024]{2,1,0:T(8,128)(2,1)S(1)}, bf16[2,64,1024]{2,1,0:T(8,128)(2,1)S(1)}, u32[]{:S(2)}, u32[]{:S(2)}) %collective-permute-start) | collective-permute-done | bytes 262176 | tf_op jit(solution)/shard_map/ppermute | solution.py:1077
  31.0 7.2 %shard_map.118 = bf16[16,240,128]{2,1,0:T(8,128)(2,1)} custom-call(s32[4]{0:T(128)} %add_add_fusion.scalars, f32[8,128]{1,0:T(8,128)} %bitcast.68, f32[3080,128]{1,0:T(8,128)} %pad_bitcast_fusion.own, f32[32,128]{1,0:T(8,128)} %bitcast.62, bf16[16,128]{1,0:T(8,128)(2,1)} %maximum_maximum_fusion.places), custom_call_target="tpu_custom_call" | custom-call | tf_op jit(solution)/shard_map/pallas_call | solution.py:1129
  38.2 50.3 %all_to_all.20.own = bf16[16,240,128]{2,1,0:T(8,128)(2,1)S(1)} all-to-all(bf16[16,240,128]{2,1,0:T(8,128)(2,1)} %shard_map.118), channel_id=1, replica_groups=mesh['x'=2,'core'=2,'z'=4,'y'=2] {'core','z','y'}, dimensions={0} | all-to-all | bytes 1966080 | tf_op jit(solution)/shard_map/all_to_all | solution.py:1137
  89.2 22.7 %collective-permute-done.5.came = bf16[16,240,128]{2,1,0:T(8,128)(2,1)S(1)} collective-permute-done((bf16[16,240,128]{2,1,0:T(8,128)(2,1)S(1)}, bf16[16,240,128]{2,1,0:T(8,128)(2,1)S(1)}, u32[]{:S(2)}, u32[]{:S(2)}) %collective-permute-start.5) | collective-permute-done | bytes 983072 | tf_op jit(solution)/shard_map/ppermute | solution.py:1077
  112.9 3.5 shard_map.121
  116.5 3.7 all-to-all-start.1
  128.6 9.6 %collective-permute-done.4.came = bf16[9,240,128]{2,1,0:T(8,128)(2,1)} collective-permute-done((bf16[9,240,128]{2,1,0:T(8,128)(2,1)}, bf16[9,240,128]{2,1,0:T(8,128)(2,1)}, u32[]{:S(2)}, u32[]{:S(2)}) %collective-permute-start.4) | collective-permute-done | bytes 552992 | tf_op jit(solution)/shard_map/ppermute | solution.py:1141
  141.2 12.4 %shard_map.120 = (bf16[2048,1024]{1,0:T(8,128)(2,1)}, bf16[2048,1024]{1,0:T(8,128)(2,1)}, bf16[2048,64]{1,0:T(8,128)(2,1)}, bf16[2048,64]{1,0:T(8,128)(2,1)}, bf...) custom-call(bf16[2,8,2,64,1024]{4,3,2,1,0:T(8,128)(2,1)} %bitcast.50, f32[2048,1]{1,0:T(8,128)} %reshape.387.place, ...), custom_call_target="tpu_custom_call" | custom-call | tf_op jit(solution)/shard_map/pallas_call | solution.py:1193
  153.7 14.6 %shard_map.122 = (bf16[2048,64]{1,0:T(8,128)(2,1)}, f32[64,2048]{1,0:T(8,128)}, f32[1,2048]{1,0:T(1,128)}) custom-call(s32[1]{0:T(128)} %dynamic_slice.34.lengths, bf16[2048,64]{1,0:T(8,128)(2,1)} %get-tuple-element.54.query, bf16[2048,64]{1,0:T(8,128)(2,1)} %get-tuple-element.55.key, bf16[2048,64]{1,0:T(8,128)(2,1)} %get-tuple-element.56.value), custom_call_target="tpu_custom_call" | custom-call | tf_op jit(solution)/shard_map/pallas_call | solution.py:1199
  171.4 16.9 %shard_map.124 = (bf16[2,8,2,64,1024]{4,3,2,1,0:T(8,128)(2,1)}, bf16[2048,64]{1,0:T(8,128)(2,1)}, bf16[2048,256]{1,0:T(8,128)(2,1)}, f32[256,1024]{1,0:T(8,128)}...) custom-call(s32[4]{0:T(128)} %pad_add_fusion.here, ...), custom_call_target="tpu_custom_call" | custom-call | tf_op jit(solution)/shard_map/pallas_call | solution.py:1212
  190.7 12.3 %shard_map.126 = (bf16[2048,64]{1,0:T(8,128)(2,1)}, bf16[2048,64]{1,0:T(8,128)(2,1)}, bf16[2048,64]{1,0:T(8,128)(2,1)}) custom-call(s32[1]{0:T(128)} %dynamic_slice.34.lengths, bf16[2048,64]{1,0:T(8,128)(2,1)} %get-tuple-element.54.query, bf16[2048,64]{1,0:T(8,128)(2,1)} %get-tuple-element.55.key, bf16[2048,64]{1,0:T(8,128)(2,1)} %get-tuple-element.56.value, ...), custom_call_target="tpu_custom_call" | custom-call | tf_op jit(solution)/shard_map/pallas_call | solution.py:1230
  203.0 13.7 %shard_map.127 = (bf16[8,2,64,1024]{3,2,1,0:T(8,128)(2,1)}, bf16[8,2,64,1024]{3,2,1,0:T(8,128)(2,1)}, f32[1024,256]{1,0:T(8,128)}, f32[1,256]{1,0:T(1,128)}, f32[8,1024]{1,0:T(8,128)}) custom-call(s32[4]{0:T(128)} %pad_add_fusion.here, bf16[2,8,2,64,1024]{4,3,2,1,0:T(8,128)(2,1)} %bitcast.51, bf16[2048,1024]{1,0:T(8,128)(2,1)} %get-tuple-element.67.one, ...), custom_call_target="tpu_custom_call" | custom-call | tf_op jit(solution)/shard_map/pallas_call | solution.py:1248
  216.8 5.9 %all-to-all-start.2 = ((bf16[16,160,128]{2,1,0:T(8,128)(2,1)}), bf16[16,160,128]{2,1,0:T(8,128)(2,1)S(1)}, u32[]{:S(2)}, u32[]{:S(2)}) async-start(bf16[16,160,128]{2,1,0:T(8,128)(2,1)} %shard_map.125), calls=%async_computation.3 | async-start | bytes 1310720 | tf_op jit(solution)/shard_map/all_to_all | solution.py:1225
  223.3 17.9 %all-to-all-done.2.second = bf16[16,160,128]{2,1,0:T(8,128)(2,1)S(1)} async-done(((bf16[16,160,128]{2,1,0:T(8,128)(2,1)}), bf16[16,160,128]{2,1,0:T(8,128)(2,1)S(1)}, u32[]{:S(2)}, u32[]{:S(2)}) %all-to-all-start.2) | async-done | bytes 655392 | tf_op jit(solution)/shard_map/all_to_all | solution.py:1225
  242.0 4.7 %shard_map.128 = (bf16[16,224,128]{2,1,0:T(8,128)(2,1)}, bf16[16,224,128]{2,1,0:T(8,128)(2,1)}) custom-call(s32[2]{0:T(128)} %pad_add_fusion.1.scalars, bf16[16,160,128]{2,1,0:T(8,128)(2,1)} %copy-done.6, f32[1024,256]{1,0:T(8,128)} %get-tuple-element.84.expand_g, f32[1,1024]{1,0:T(1,128)} %broadcast_select_fusion.bias_g, f32[1,256]{1,0:T(1,128)} %get-tuple-element.86.expand_bg), custom_call_target="tpu_custom_call" | custom-call | tf_op jit(solution)/shard_map/pallas_call | solution.py:1240
  246.7 11.6 %collective-permute-start.12 = (bf16[16,224,128]{2,1,0:T(8,128)(2,1)}, bf16[16,224,128]{2,1,0:T(8,128)(2,1)S(1)}, u32[]{:S(2)}, u32[]{:S(2)}) collective-permute-start(bf16[16,224,128]{2,1,0:T(8,128)(2,1)} %get-tuple-element.88), channel_id=1, source_target_pairs={{0,16},{16,0},{1,17},{17,1},{2,18},{18,2},{3,19},{19,3},{4,20},{20... | collective-permute-start | bytes 2752520 | tf_op jit(solution)/shard_map/ppermute | solution.py:1077
  258.3 4.2 %add_convert_fusion.1 = (bf16[4,2,64,1024]{3,2,1,0:T(8,128)(2,1)S(1)}, bf16[4,2,64,1024]{3,2,1,0:T(8,128)(2,1)}) fusion(bf16[8,2,64,1024]{3,2,1,0:T(8,128)(2,1)} %collective-permute-done.7, bf16[8,2,64,1024]{3,2,1,0:T(8,128)(2,1)} %get-tuple-element.80), kind=kLoop, calls=%fused_computation.1 | loop fusion | flops 4194304 | bytes 6291456 | tf_op jit(solution)/shard_map/convert_element_type | solution.py:1177
  267.3 19.3 %collective-permute-done.13.late_came = bf16[1600,128]{1,0:T(8,128)(2,1)S(1)} collective-permute-done((bf16[1600,128]{1,0:T(8,128)(2,1)}, bf16[1600,128]{1,0:T(8,128)(2,1)S(1)}, u32[]{:S(2)}, u32[]{:S(2)}) %collective-permute-start.13) | collective-permute-done | bytes 409632 | tf_op jit(solution)/shard_map/ppermute | solution.py:1266
  290.6 4.3 %all-to-all-start.3 = ((bf16[16,224,128]{2,1,0:T(8,128)(2,1)}), bf16[16,224,128]{2,1,0:T(8,128)(2,1)}, u32[]{:S(2)}, u32[]{:S(2)}) async-start(bf16[16,224,128]{2,1,0:T(8,128)(2,1)} %shard_map.130), calls=%async_computation.4 | async-start | bytes 1835008 | tf_op jit(solution)/shard_map/all_to_all | solution.py:1273
  300.1 23.8 %collective-permute-done.9 = bf16[2,2,64,1024]{3,2,1,0:T(8,128)(2,1)S(1)} collective-permute-done((bf16[2,2,64,1024]{3,2,1,0:T(8,128)(2,1)}, bf16[2,2,64,1024]{3,2,1,0:T(8,128)(2,1)S(1)}, u32[]{:S(2)}, u32[]{:S(2)}) %collective-permute-start.9) | collective-permute-done | bytes 524320 | tf_op jit(solution)/shard_map/ppermute | solution.py:1172
  327.4 7.9 %shard_map.131 = f32[3120,128]{1,0:T(8,128)} custom-call(s32[4]{0:T(128)} %add_add_fusion.1.scalars, bf16[16,224,128]{2,1,0:T(8,128)(2,1)} %all-to-all-done.3.got), custom_call_target="tpu_custom_call" | custom-call | tf_op jit(solution)/shard_map/pallas_call | solution.py:1276
  338.2 4.5 %collective-permute-start.14 = (f32[4096]{0:T(1024)S(1)}, f32[4096]{0:T(1024)S(1)}, u32[]{:S(2)}, u32[]{:S(2)}) collective-permute-start(f32[4096]{0:T(1024)S(1)} %slice.121), channel_id=1, source_target_pairs={{0,1},{1,2},{2,3},{3,4},{4,5},{5,6},{6,7},{7,8},{8,9},{9,10},{10,1... | collective-permute-start | bytes 49160 | tf_op jit(solution)/shard_map/ppermute | solution.py:1280
  344.2 4.5 %add_multiply_fusion = (f32[393632]{0:T(1024)}, f32[393632]{0:T(1024)}, f32[393632]{0:T(1024)}, f32[393632]{0:T(1024)}) fusion(f32[393632]{0:T(1024)S(1)} %copy-done.7, f32[393632]{0:T(1024)S(1)} %copy-done.3, f32[393632]{0:T(1024)} %param.12, f32[1024]{0:T(1024)S(1)} %collective-permute-done.15, f32[4096]{0:T(1024)S(1)} %collective-permute-done.14, ...), kind=kLoop, calls=%fused_computation.4 | loop fusion | flops 3936320 | bytes 12616704 | tf_op jit(solution)/shard_map/add | solution.py:1301
  348.9 48.6 %reduce-scatter.2.cloned.1.call-done = bf16[1,2,64,1024]{3,2,1,0:T(8,128)(2,1)} async-done(((bf16[16,2,64,1024]{3,2,1,0:T(8,128)(2,1)}), bf16[1,2,64,1024]{3,2,1,0:T(8,128)(2,1)}) %reduce-scatter.2.cloned.1.call-update) | async-done | bytes 262160 | tf_op jit(solution)/shard_map/reduce_scatter | solution.py:1226
  (117 shorter events, 66.3 us)
Async XLA Ops:
  7.2 134.1 %all-gather.5.cloned.1.call-start = ((), (), s32[]{:S(2)}) async-start(), calls=%async_computation.6 | async-start | bytes 4456448 | tf_op jit(solution)/shard_map/all_gather | solution.py:1100
  8.4 9.3 %collective-permute-start = (bf16[2,64,1024]{2,1,0:T(8,128)(2,1)S(1)}, bf16[2,64,1024]{2,1,0:T(8,128)(2,1)S(1)}, u32[]{:S(2)}, u32[]{:S(2)}) collective-permute-start(bf16[2,64,1024]{2,1,0:T(8,128)(2,1)S(1)} %get-tuple-element.105), channel_id=1, source_target_pairs={{0,16},{16,0},{1,17},{17,1},{2,18},{18,2},{3,19},{19,3},{4,20},{20... | collective-permute-start | bytes 786440 | tf_op jit(solution)/shard_map/ppermute | solution.py:1077
  18.7 152.7 %all-gather.7.cloned.1.call-start = ((), (), s32[]{:S(2)}) async-start(), calls=%async_computation.7 | async-start | bytes 4456448 | tf_op jit(solution)/shard_map/all_gather | solution.py:1101
  19.4 8.6 %collective-permute-start.3 = (s32[64]{0:T(128)S(1)}, s32[64]{0:T(128)S(1)}, u32[]{:S(2)}, u32[]{:S(2)}) collective-permute-start(s32[64]{0:T(128)S(1)} %get-tuple-element.117), channel_id=1, source_target_pairs={{0,16},{16,0},{1,17},{17,1},{2,18},{18,2},{3,19},{19,3},{4,20},{20... | collective-permute-start | bytes 776 | tf_op jit(solution)/shard_map/ppermute | solution.py:1077
  21.3 7.5 %collective-permute-start.1 = (f32[1024]{0:T(1024)S(1)}, f32[1024]{0:T(1024)S(1)}, u32[]{:S(2)}, u32[]{:S(2)}) collective-permute-start(f32[1024]{0:T(1024)S(1)} %slice.79), channel_id=1, source_target_pairs={{0,1},{1,2},{2,3},{3,4},{4,5},{5,6},{6,7},{7,8},{8,9},{9,10},{10,1... | collective-permute-start | bytes 12296 | tf_op jit(solution)/shard_map/ppermute | solution.py:1110
  24.8 5.6 %collective-permute-start.2 = (f32[4096]{0:T(1024)S(1)}, f32[4096]{0:T(1024)S(1)}, u32[]{:S(2)}, u32[]{:S(2)}) collective-permute-start(f32[4096]{0:T(1024)S(1)} %slice.80), channel_id=1, source_target_pairs={{1,0},{2,1},{3,2},{4,3},{5,4},{6,5},{7,6},{8,7},{9,8},{10,9},{11,1... | collective-permute-start | bytes 49160 | tf_op jit(solution)/shard_map/ppermute | solution.py:1111
  88.5 23.5 %collective-permute-start.5 = (bf16[16,240,128]{2,1,0:T(8,128)(2,1)S(1)}, bf16[16,240,128]{2,1,0:T(8,128)(2,1)S(1)}, u32[]{:S(2)}, u32[]{:S(2)}) collective-permute-start(bf16[16,240,128]{2,1,0:T(8,128)(2,1)S(1)} %all_to_all.20.own), channel_id=1, source_target_pairs={{0,16},{16,0},{1,17},{17,1},{2,18},{18,2},{3,19},{19,3},{4,20},{20... | collective-permute-start | bytes 2949128 | tf_op jit(solution)/shard_map/ppermute | solution.py:1077
  89.2 30.9 %copy-start.16 = (s32[2]{0:T(128)S(1)}, s32[2]{0:T(128)}, u32[]{:S(2)}) copy-start(s32[2]{0:T(128)} %param.9) | copy-start | bytes 28
  116.5 51.9 %all-to-all-start.1 = ((bf16[16,160,128]{2,1,0:T(8,128)(2,1)}), bf16[16,160,128]{2,1,0:T(8,128)(2,1)S(1)}, u32[]{:S(2)}, u32[]{:S(2)}) async-start(bf16[16,160,128]{2,1,0:T(8,128)(2,1)} %get-tuple-element.53), calls=%async_computation.1 | async-start | bytes 1310720 | tf_op jit(solution)/shard_map/all_to_all | solution.py:1157
  123.5 14.8 %collective-permute-start.4 = (bf16[9,240,128]{2,1,0:T(8,128)(2,1)}, bf16[9,240,128]{2,1,0:T(8,128)(2,1)}, u32[]{:S(2)}, u32[]{:S(2)}) collective-permute-start(bf16[9,240,128]{2,1,0:T(8,128)(2,1)} %slice.108), channel_id=1, source_target_pairs={{0,16},{1,17},{2,18},{3,19},{4,20},{5,21},{6,22},{7,23},{8,24},{9,... | collective-permute-start | bytes 1658888 | tf_op jit(solution)/shard_map/ppermute | solution.py:1141
  216.7 41.6 %collective-permute-start.7 = (bf16[8,2,64,1024]{3,2,1,0:T(8,128)(2,1)}, bf16[8,2,64,1024]{3,2,1,0:T(8,128)(2,1)}, u32[]{:S(2)}, u32[]{:S(2)}) collective-permute-start(bf16[8,2,64,1024]{3,2,1,0:T(8,128)(2,1)} %get-tuple-element.81), channel_id=1, source_target_pairs={{0,8},{8,0},{1,9},{9,1},{2,10},{10,2},{3,11},{11,3},{4,12},{12,4},... | collective-permute-start | bytes 6291464 | tf_op jit(solution)/shard_map/ppermute | solution.py:1172
  216.8 24.4 %all-to-all-start.2 = ((bf16[16,160,128]{2,1,0:T(8,128)(2,1)}), bf16[16,160,128]{2,1,0:T(8,128)(2,1)S(1)}, u32[]{:S(2)}, u32[]{:S(2)}) async-start(bf16[16,160,128]{2,1,0:T(8,128)(2,1)} %shard_map.125), calls=%async_computation.3 | async-start | bytes 1310720 | tf_op jit(solution)/shard_map/all_to_all | solution.py:1225
  246.7 40.0 %collective-permute-start.12 = (bf16[16,224,128]{2,1,0:T(8,128)(2,1)}, bf16[16,224,128]{2,1,0:T(8,128)(2,1)S(1)}, u32[]{:S(2)}, u32[]{:S(2)}) collective-permute-start(bf16[16,224,128]{2,1,0:T(8,128)(2,1)} %get-tuple-element.88), channel_id=1, source_target_pairs={{0,16},{16,0},{1,17},{17,1},{2,18},{18,2},{3,19},{19,3},{4,20},{20... | collective-permute-start | bytes 2752520 | tf_op jit(solution)/shard_map/ppermute | solution.py:1077
  262.5 32.8 %collective-permute-start.8 = (bf16[4,2,64,1024]{3,2,1,0:T(8,128)(2,1)}, bf16[4,2,64,1024]{3,2,1,0:T(8,128)(2,1)}, u32[]{:S(2)}, u32[]{:S(2)}) collective-permute-start(bf16[4,2,64,1024]{3,2,1,0:T(8,128)(2,1)} %get-tuple-element.99), channel_id=1, source_target_pairs={{0,1},{1,0},{2,3},{3,2},{4,5},{5,4},{6,7},{7,6},{8,9},{9,8},{10,11... | collective-permute-start | bytes 3145736 | tf_op jit(solution)/shard_map/ppermute | solution.py:1172
  265.9 20.8 %collective-permute-start.13 = (bf16[1600,128]{1,0:T(8,128)(2,1)}, bf16[1600,128]{1,0:T(8,128)(2,1)S(1)}, u32[]{:S(2)}, u32[]{:S(2)}) collective-permute-start(bf16[1600,128]{1,0:T(8,128)(2,1)} %shard_map.129.late), channel_id=1, source_target_pairs={{16,0},{17,1},{18,2},{19,3},{20,4},{21,5},{22,6},{23,7},{24,8},{25... | collective-permute-start | bytes 1228808 | tf_op jit(solution)/shard_map/ppermute | solution.py:1266
  290.6 36.7 %all-to-all-start.3 = ((bf16[16,224,128]{2,1,0:T(8,128)(2,1)}), bf16[16,224,128]{2,1,0:T(8,128)(2,1)}, u32[]{:S(2)}, u32[]{:S(2)}) async-start(bf16[16,224,128]{2,1,0:T(8,128)(2,1)} %shard_map.130), calls=%async_computation.4 | async-start | bytes 1835008 | tf_op jit(solution)/shard_map/all_to_all | solution.py:1273
  295.0 102.6 %reduce-scatter.2.cloned.1.call-start = ((), (), s32[]{:S(2)}) async-start(), calls=%async_computation.5 | async-start | bytes 4456448 | tf_op jit(solution)/shard_map/reduce_scatter | solution.py:1226
  297.7 26.3 %collective-permute-start.9 = (bf16[2,2,64,1024]{3,2,1,0:T(8,128)(2,1)}, bf16[2,2,64,1024]{3,2,1,0:T(8,128)(2,1)S(1)}, u32[]{:S(2)}, u32[]{:S(2)}) collective-permute-start(bf16[2,2,64,1024]{3,2,1,0:T(8,128)(2,1)} %get-tuple-element.101), channel_id=1, source_target_pairs={{0,2},{2,0},{4,6},{6,4},{1,3},{3,1},{5,7},{7,5},{8,10},{10,8},{12,... | collective-permute-start | bytes 1572872 | tf_op jit(solution)/shard_map/ppermute | solution.py:1172
  324.0 18.7 %collective-permute-start.10 = (bf16[1,2,64,1024]{3,2,1,0:T(8,128)(2,1)S(1)}, bf16[1,2,64,1024]{3,2,1,0:T(8,128)(2,1)S(1)}, u32[]{:S(2)}, u32[]{:S(2)}) collective-permute-start(bf16[1,2,64,1024]{3,2,1,0:T(8,128)(2,1)S(1)} %add_convert_fusion.5), channel_id=1, source_target_pairs={{0,4},{4,0},{2,6},{6,2},{1,5},{5,1},{3,7},{7,3},{8,12},{12,8},{10,... | collective-permute-start | bytes 786440 | tf_op jit(solution)/shard_map/ppermute | solution.py:1172
  336.1 7.7 %collective-permute-start.15 = (f32[1024]{0:T(1024)S(1)}, f32[1024]{0:T(1024)S(1)}, u32[]{:S(2)}, u32[]{:S(2)}) collective-permute-start(f32[1024]{0:T(1024)S(1)} %slice_bitcast_fusion), channel_id=1, source_target_pairs={{1,0},{2,1},{3,2},{4,3},{5,4},{6,5},{7,6},{8,7},{9,8},{10,9},{11,1... | collective-permute-start | bytes 12296 | tf_op jit(solution)/shard_map/ppermute | solution.py:1281
  338.2 6.0 %collective-permute-start.14 = (f32[4096]{0:T(1024)S(1)}, f32[4096]{0:T(1024)S(1)}, u32[]{:S(2)}, u32[]{:S(2)}) collective-permute-start(f32[4096]{0:T(1024)S(1)} %slice.121), channel_id=1, source_target_pairs={{0,1},{1,2},{2,3},{3,4},{4,5},{5,6},{6,7},{7,8},{8,9},{9,10},{10,1... | collective-permute-start | bytes 49160 | tf_op jit(solution)/shard_map/ppermute | solution.py:1280
  342.9 60.6 %copy-start.8 = (bf16[2,64,1024]{2,1,0:T(8,128)(2,1)S(1)}, bf16[2,64,1024]{2,1,0:T(8,128)(2,1)}, u32[]{:S(2)}) copy-start(bf16[2,64,1024]{2,1,0:T(8,128)(2,1)} %param.8) | copy-start | bytes 786436
  342.9 5.7 %collective-permute-start.11 = (bf16[64,1024]{1,0:T(8,128)(2,1)S(1)}, bf16[64,1024]{1,0:T(8,128)(2,1)S(1)}, u32[]{:S(2)}, u32[]{:S(2)}) collective-permute-start(bf16[64,1024]{1,0:T(8,128)(2,1)S(1)} %get-tuple-element.108), channel_id=1, source_target_pairs={{0,16},{16,0},{1,17},{17,1},{2,18},{18,2},{3,19},{19,3},{4,20},{20... | collective-permute-start | bytes 393224 | tf_op jit(solution)/shard_map/ppermute | solution.py:1077
  398.5 5.0 %collective-permute-start.6 = (bf16[64,1024]{1,0:T(8,128)(2,1)S(1)}, bf16[64,1024]{1,0:T(8,128)(2,1)S(1)}, u32[]{:S(2)}, u32[]{:S(2)}) collective-permute-start(bf16[64,1024]{1,0:T(8,128)(2,1)S(1)} %get-tuple-element.111), channel_id=1, source_target_pairs={{0,16},{16,0},{1,17},{17,1},{2,18},{18,2},{3,19},{19,3},{4,20},{20... | collective-permute-start | bytes 393224 | tf_op jit(solution)/shard_map/ppermute | solution.py:1077
  (15 other events, 110.1 us)
Sparse Core Ops, SparseCore 0:
  18.8 68.8 all-gather.4
  90.5 58.7 all-gather.6
  327.5 70.0 reduce-scatter.1
where the time goes:
time: 413 us; the launch traced here: 411 us
  waiting for transfers between devices  155 us (38%)
  Pallas kernels  107 us (26%)
  starting transfers between devices  52.5 us (13%)
  blocking collectives  50.3 us (12%)
  other arithmetic  20.1 us (5%)
  between operations  14.1 us (3%)
  local copies, waits for them, and re-layouts  12.8 us (3%)
    all_to_all x1, blocking collectives, by_head(): got = lax.all_to_all(sent, RING, 0, 0, tiled=True)  50.3 us
    reduce_scatter x1, waiting for transfers between devices, by_head(): lax.psum_scatter(partial_out.reshape(16, 2, span, width), RING, scatter_d...  48.6 us
    ppermute x6, waiting for transfers between devices, across_x(): return lax.ppermute(block, 'x', [(0, 1), (1, 0)])  32.6 us
    ppermute x4, waiting for transfers between devices, summed(): came = lax.ppermute(sent, axis, route)  23.8 us
    ppermute x1, waiting for transfers between devices, by_head(): late_came = lax.ppermute(late, 'x', [(1, 0)])  19.3 us
    ppermute x6, starting transfers between devices, across_x(): return lax.ppermute(block, 'x', [(0, 1), (1, 0)])  18.9 us
    all_to_all x1, waiting for transfers between devices, by_head(): second_g = lax.all_to_all(second_g, RING, 0, 0, tiled=True)  17.9 us
    pallas_call x1, Pallas kernels, by_head(): call(feed_body, steps, [rows_spec(D), rows_spec(HD), token_spec, whole((D...  16.9 us
  transfers between devices with their start and end apart: 22, of which 10 were waited for; matrix products, arithmetic and copies ran while one was open for 6% of the time, Pallas kernels for 15%

commit v1 on v0

--- a/solution.py
+++ b/solution.py
@@ -524,12 +524,13 @@
 
 
 SHIFT_ROWS = 3200
+START, SHIFT, KIND, VECTOR, START_BACK, SHIFT_BACK, HEAD, X, LENGTH, CORE, Y, Z = range(12)
 SEND_ROWS = PIECE + 32 + 16
 OWN_ROW = 64
 
 
 def weights_out_body(scalars, before, own, after, places, out, source, flat, tail):
-    start, shift, kind, vector_row = scalars[0], scalars[1], scalars[2], scalars[3]
+    start, shift, kind, vector_row = scalars[START], scalars[SHIFT], scalars[KIND], scalars[VECTOR]
     count = own.shape[0]
     source[0 : OWN_ROW - 8] = jnp.zeros((OWN_ROW - 8, LANES), F32)
     source[OWN_ROW - 8 : OWN_ROW] = before[...]
@@ -613,40 +614,20 @@
         vectors[to : to + 1, 128 * j : 128 * j + 128] = tile[j : j + 1]
 
 
-def project_in_body(scalars, own, came, qkv_w, vectors, qkv_b, project_rows):
-    head = scalars[0]
+def weights_in_body(facts, own, came, qkv_w, expand_w, second, vectors, qkv_b, expand_b, places, held, rows):
+    head = facts[HEAD]
     low = low_lanes((64, LANES))
     vectors[...] = jnp.zeros(vectors.shape, F32)
 
-    def take(got):
+    def take(lower, upper, slot):
+        def block(c, at, count):
+            return (lower if c < 16 else upper)[c % 16, at : at + count]
+
         for c in range(8):
-            qkv_w[128 * c : 128 * c + 128, 0:128] = got[c, 0:128]
-            packed = got[c, 128:192].astype(F32)
+            qkv_w[128 * c : 128 * c + 128, 0:128] = block(c, 0, 128)
+            packed = block(c, 128, 64).astype(F32)
             qkv_w[128 * c : 128 * c + 64, 128:256] = jnp.where(low, packed, 0.0).astype(BF16)
             qkv_w[128 * c + 64 : 128 * c + 128, 128:256] = jnp.where(low, swap(packed), 0.0).astype(BF16)
-        project_rows[0:32] = got[0, PIECE : PIECE + 32].astype(F32)
-        for v in range(4):
-            spread(project_rows, 8 * v, vectors, v)
-        project_rows[0:24] = got[8, PIECE + 8 : PIECE + 32].astype(F32)
-
-    pl.when(scalars[1] == 0)(lambda: take(own))
-    pl.when(scalars[1] != 0)(lambda: take(came))
-    row = head // 2 * 3
-    first, middle, last = (project_rows[pl.ds(row + j, 1), :] for j in range(3))
-    odd = head % 2 == 1
-    qkv_b[0:1, 0:128] = jnp.where(odd, join(middle, 1, last, 0), first)
-    value = jnp.where(odd, swap(last), middle)
-    qkv_b[0:1, 128:256] = jnp.where(low_lanes((1, LANES)), value, 0.0)
-
-
-def rest_in_body(scalars, own, came, expand_w, second, biases, expand_b, rows):
-    head = scalars[0]
-    biases[...] = jnp.zeros(biases.shape, F32)
-
-    def take(lower, upper):
-        def block(c, at, count):
-            return (lower if c < 16 else upper)[c % 16, at : at + count]
-
         for c, at, row, count in expand_places():
             expand_w[row : row + count, 0:128] = block(c, at, count)
             expand_w[row : row + count, 128:256] = block(c, at + count, count)
@@ -662,13 +643,29 @@
                 a, half = tile(shrink_place(256 * h + 64 * part))
                 b, other = tile(shrink_place(256 * h + 128 + 64 * part))
                 second[h, 32 + 64 * part : 96 + 64 * part] = join(a, half, b, other).astype(BF16)
-        for to, c in enumerate((10, 31)):
+        for group in range(8):
+            for x in range(2):
+                a, b = (block(16 * x + 8 * core + group, PIECE + 32, 16).astype(F32) for core in range(2))
+                a, b = (t[0:1] * 256.0 + t[1:2] for t in (a, b))
+                row = 2 * group + x
+                places[row : row + 1] = join(a, slot, b, slot)
+        held[...] = block(0, PIECE, 32).astype(F32)
+        for v in range(4):
+            spread(held, 8 * v, vectors, v)
+        for to, c in ((4, 10), (5, 31)):
             rows[0:16] = block(c, PIECE, 16).astype(F32)
-            spread(rows, 0, biases, to)
+            spread(rows, 0, vectors, to)
+        held[0:24] = block(8, PIECE, 32)[8:].astype(F32)
         rows[...] = block(21, PIECE, 32).astype(F32)
 
-    pl.when(scalars[1] == 0)(lambda: take(own, came))
-    pl.when(scalars[1] != 0)(lambda: take(came, own))
+    pl.when(facts[X] == 0)(lambda: take(own, came, 0))
+    pl.when(facts[X] != 0)(lambda: take(came, own, 1))
+    row = head // 2 * 3
+    first, middle, last = (held[pl.ds(row + j, 1), :] for j in range(3))
+    odd = head % 2 == 1
+    qkv_b[0:1, 0:128] = jnp.where(odd, join(middle, 1, last, 0), first)
+    value = jnp.where(odd, swap(last), middle)
+    qkv_b[0:1, 128:256] = jnp.where(low_lanes((1, LANES)), value, 0.0)
     expand_b[0:1, 0:128] = rows[pl.ds(2 * head, 1), :]
     expand_b[0:1, 128:256] = rows[pl.ds(2 * head + 1, 1), :]
 
@@ -693,7 +690,7 @@
 
 
 def early_body(scalars, second, expand_g, bias_g, expand_bg, own, other, expand_rows):
-    head = scalars[0]
+    head = scalars[HEAD]
     expand_rows[...] = jnp.zeros(expand_rows.shape, F32)
     expand_rows[pl.ds(2 * head, 1), :] = expand_bg[0:1, 0:128]
     expand_rows[pl.ds(2 * head + 1, 1), :] = expand_bg[0:1, 128:256]
@@ -735,15 +732,15 @@
         store(31, PIECE, bias)
         store(21, PIECE, expand_rows[...].astype(BF16))
 
-    pl.when(scalars[1] == 0)(lambda: put(own, other))
-    pl.when(scalars[1] != 0)(lambda: put(other, own))
+    pl.when(scalars[X] == 0)(lambda: put(own, other))
+    pl.when(scalars[X] != 0)(lambda: put(other, own))
 
 
 LATE_ROWS = 8 * PIECE + 64
 
 
 def late_body(scalars, qkv_g, vector_g, qkv_bg, out, project_rows):
-    head = scalars[0]
+    head = scalars[HEAD]
     for c in range(8):
         at = PIECE * c
         out[at : at + 128] = qkv_g[128 * c : 128 * c + 128, 0:128].astype(BF16)
@@ -772,7 +769,7 @@
 
     lax.fori_loop(0, 16, add, 0)
 
-    @pl.when(scalars[0] == 0)
+    @pl.when(scalars[X] == 0)
     def _():
         def total(at, count):
             return (late[at : at + count].astype(F32) + late_came[at : at + count].astype(F32)).astype(BF16)
@@ -788,7 +785,7 @@
 
 
 def grads_in_body(scalars, got, out, flat):
-    start, shift, kind, vector_row = scalars[0], scalars[1], scalars[2], scalars[3]
+    start, shift, kind, vector_row = scalars[START_BACK], scalars[SHIFT_BACK], scalars[KIND], scalars[VECTOR]
     lead = LEAD + 8
 
     def clear(step, carry):
@@ -870,8 +867,8 @@
 
 
 def relative_place(i, here):
-    y = (i & 1) ^ here[2]
-    z = (i >> 1) ^ here[3]
+    y = (i & 1) ^ here[Y]
+    z = (i >> 1) ^ here[Z]
     return y * 4 + (z & 1) * 2 + (z >> 1)
 
 
@@ -890,9 +887,11 @@
     return pair * cos + other * sin
 
 
-def mixed_body(tokens, place, vectors, qkv_w, qkv_b, inverse, one, two, query, key, value, cos, sin):
+def mixed_body(tokens, places, vectors, qkv_w, qkv_b, inverse, one, two, query, key, value, cos, sin):
     unit = normalized(token_rows(tokens).astype(F32))
-    angles = place[...] * inverse[...]
+    at = 2 * pl.program_id(0)
+    place = [jnp.broadcast_to(places[pl.ds(at + x, 1), :], (LANES, LANES)).T for x in range(2)]
+    angles = jnp.concatenate(place, axis=0) * inverse[...]
     cos[...] = jnp.cos(angles)
     sin[...] = jnp.sin(angles)
     first = (unit * vectors[0:1] + vectors[1:2]).astype(BF16)
@@ -921,7 +920,7 @@
 
 def attend_body(lengths, query, key, value, low_out, full_out, log_out, scores, value_t):
     at = pl.program_id(0)
-    length = lengths[0]
+    length = lengths[LENGTH]
 
     @pl.when(at == 0)
     def _():
@@ -965,7 +964,7 @@
     lengths, query, key, value, grad, full_out, log_in, query_g, key_g, value_g, key_t, key_sum, value_sum
 ):
     at = pl.program_id(0)
-    length = lengths[0]
+    length = lengths[LENGTH]
 
     @pl.when(at == 0)
     def _():
@@ -1027,7 +1026,7 @@
     for i, (core, x) in enumerate(((0, 0), (1, 0), (0, 1), (1, 1))):
         partial_out[core, 0, x] = partial[step * i : step * i + step].astype(BF16)
     token = at * BLOCK + lax.broadcasted_iota(jnp.int32, (BLOCK, D), 0)
-    seed = jnp.where(token < here[0], token_rows(cotangent).astype(F32), 0.0)
+    seed = jnp.where(token < here[LENGTH], token_rows(cotangent).astype(F32), 0.0)
     bias_g[...] += jnp.sum(seed, axis=0, keepdims=True)
     seed = seed.astype(BF16)
     attended_g[...] = mm(seed, dense_w[...], ((1,), (1,))).astype(BF16)
@@ -1065,7 +1064,7 @@
     vector_g[1:2] += jnp.sum(one_g, axis=0, keepdims=True)
     vector_g[2:3] += jnp.sum(two_g * unit, axis=0, keepdims=True)
     vector_g[3:4] += jnp.sum(two_g, axis=0, keepdims=True)
-    put_rows(kept, sent, one_g * vectors[0:1] + two_g * vectors[2:3], here[1])
+    put_rows(kept, sent, one_g * vectors[0:1] + two_g * vectors[2:3], here[CORE])
 
 
 def split_mesh(mesh):
@@ -1095,7 +1094,7 @@
 
     rows = jnp.stack([residual, cotangent], axis=1)
     rows = paired(at_x(rows, x), across_x(at_x(rows, 1 - x)))
-    places = paired(at_x(positions, x), across_x(at_x(positions, 1 - x))).reshape(1, 2 * span)
+    places = positions.reshape(1, 2 * span)
     tokens_shape = (2, groups, 2, span, width)
     slot_tokens = lax.all_gather(rows[:, 0], RING, axis=0).reshape(tokens_shape)
     slot_cotangent = lax.all_gather(rows[:, 1], RING, axis=0).reshape(tokens_shape)
@@ -1125,7 +1124,10 @@
     vector_row = jnp.where(owner == 10, 2080, jnp.where(owner == 21, 1056, jnp.where(owner == 31, 3104, 0)))
     ahead = skipped * D - (chunk - PER * D) * owner
     begin = ahead + 4 * D
-    scalars = jnp.stack([begin // LANES, begin % LANES, kind, vector_row]).astype(jnp.int32)
+    begin_g = (chunk - PER * D) * owner - skipped * D + 4 * D
+    y, z, core = lax.axis_index("y"), lax.axis_index("z"), lax.axis_index("core")
+    facts = [begin // LANES, begin % LANES, kind, vector_row, begin_g // LANES, begin_g % LANES]
+    facts = jnp.stack(facts + [head, x, length[0], core, y, z]).astype(jnp.int32)
     sent = call(
         weights_out_body, (1,),
         [whole(before.shape), whole(own.shape), whole(after.shape), whole(places.shape)],
@@ -1133,35 +1135,23 @@
         shaped((16, SEND_ROWS, LANES), BF16),
         [pltpu.VMEM((3280, LANES), F32), pltpu.VMEM((SHIFT_ROWS, LANES), F32), pltpu.VMEM((48, LANES), F32)],
         1,
-    )(scalars, before, own, after, places)
+    )(facts, before, own, after, places)
     got = lax.all_to_all(sent, RING, 0, 0, tiled=True)
-    head_scalar = jnp.stack([head, x]).astype(jnp.int32)
-    place = got[:, PIECE + 32 : PIECE + 34].astype(F32).reshape(2, groups, 2, 2, span)
-    place = (place[:, :, 0] * 256.0 + place[:, :, 1]).transpose(1, 2, 0, 3).reshape(count, 1)
-    came = lax.ppermute(got[:9], "x", [(0, 1)])
-    qkv_w, vectors, qkv_b = call(
-        project_in_body, (1,),
-        [whole((9, SEND_ROWS, LANES)), whole((9, SEND_ROWS, LANES))],
-        [whole((D, 256)), whole((8, D)), whole((1, 256))],
-        [shaped((D, 256), BF16), shaped((8, D), F32), shaped((1, 256), F32)],
-        [pltpu.VMEM((32, LANES), F32)], 1,
-    )(head_scalar, got, came)
     came = across_x(got)
-    expand_w, second, biases, expand_b = call(
-        rest_in_body, (1,),
+    qkv_w, expand_w, second, vectors, qkv_b, expand_b, places = call(
+        weights_in_body, (1,),
         [whole(got.shape), whole(got.shape)],
-        [whole((D, 256)), whole((16, 160, LANES)), whole((8, D)), whole((1, 256))],
-        [shaped((D, 256), BF16), shaped((16, 160, LANES), BF16), shaped((8, D), F32), shaped((1, 256), F32)],
-        [pltpu.VMEM((32, LANES), F32)], 1,
-    )(head_scalar, got, came)
+        [whole((D, 256)), whole((D, 256)), whole((16, 160, LANES)), whole((8, D)), whole((1, 256)), whole((1, 256)),
+         whole((16, LANES))],
+        [shaped((D, 256), BF16), shaped((D, 256), BF16), shaped((16, 160, LANES), BF16), shaped((8, D), F32),
+         shaped((1, 256), F32), shaped((1, 256), F32), shaped((16, LANES), F32)],
+        [pltpu.VMEM((32, LANES), F32), pltpu.VMEM((32, LANES), F32)], 1,
+    )(facts, got, came)
     second = lax.all_to_all(second, RING, 0, 0, tiled=True)
     steps = (count // BLOCK,)
     token_spec = pl.BlockSpec((2, 1, 2, span, width), lambda i, *_: (0, i, 0, 0, 0))
     part_spec = pl.BlockSpec((1, 2, span, width), lambda i, here: (relative_place(i, here), 0, 0, 0))
     part_shape = shaped((groups, 2, span, width), BF16)
-    y, z, core = lax.axis_index("y"), lax.axis_index("z"), lax.axis_index("core")
-    here = jnp.stack([length[0], core, y, z]).astype(jnp.int32)
-
     swap_pair, far_pairs = [(0, 1), (1, 0)], [(0, 2), (2, 0), (1, 3), (3, 1)]
 
     def summed(kept, sent):
@@ -1192,17 +1182,17 @@
     table = shaped((count, LANES), F32)
     one, two, query, key, value, cos, sin = call(
         mixed_body, steps,
-        [token_spec, rows_spec(1), whole((8, D)), whole((D, 256)), whole((1, 256)), whole((1, LANES))],
+        [token_spec, whole((16, LANES)), whole((8, D)), whole((D, 256)), whole((1, 256)), whole((1, LANES))],
         [rows_spec(D), rows_spec(D), rows_spec(HD), rows_spec(HD), rows_spec(HD), rows_spec(LANES), rows_spec(LANES)],
         [shaped((count, D), BF16), shaped((count, D), BF16), narrow, narrow, narrow, table, table],
-    )(slot_tokens, place, vectors, qkv_w, qkv_b, inverse)
+    )(slot_tokens, places, vectors, qkv_w, qkv_b, inverse)
     attended, attended_full, log_total = call(
         attend_body, steps,
         [rows_spec(HD), whole((count, HD)), whole((count, HD))],
         [rows_spec(HD), columns_spec(HD), columns_spec(1)],
         [narrow, shaped((HD, count), F32), shaped((1, count), F32)],
         [pltpu.VMEM((count, BLOCK), F32), pltpu.VMEM((HD, count), BF16)], 1,
-    )(length, query, key, value)
+    )(facts, query, key, value)
     second, attended = lax.optimization_barrier((second, attended))
     dense_w, shrink_w = call(
         rows_in_body, (1,), [whole(second.shape)], [whole((HD, D)), whole((256, D))],
@@ -1216,7 +1206,7 @@
          whole((1, 256)), whole((1, D))],
         [shaped(tokens_shape, BF16), narrow, shaped((count, 256), BF16), shaped((256, D), F32), shaped((HD, D), F32),
          shaped((D, 256), F32), shaped((1, 256), F32), shaped((1, D), F32)], (), 1,
-    )(here, two, attended, slot_cotangent, expand_w, expand_b, shrink_w, dense_w)
+    )(facts, two, attended, slot_cotangent, expand_w, expand_b, shrink_w, dense_w)
     second_g = call(
         rows_out_body, (1,), [whole((HD, D)), whole((256, D))], whole((16, 160, LANES)),
         shaped((16, 160, LANES), BF16),
@@ -1234,7 +1224,7 @@
         [narrow, narrow, narrow],
         [pltpu.VMEM((HD, count), BF16), pltpu.VMEM((count, HD), F32), pltpu.VMEM((count, HD), F32)],
         1,
-    )(length, query, key, value, attended_g, attended_full, log_total)
+    )(facts, query, key, value, attended_g, attended_full, log_total)
     bias_g = jnp.where(head == 0, bias_g, 0.0)
     plane = (16, BACK_ROWS, LANES)
     early, early_other = call(
@@ -1243,7 +1233,7 @@
         [whole(plane), whole(plane)],
         [shaped(plane, BF16), shaped(plane, BF16)],
         [pltpu.VMEM((32, LANES), F32)], 1,
-    )(head_scalar, second_g, expand_g, bias_g, expand_bg)
+    )(facts, second_g, expand_g, bias_g, expand_bg)
     early_came = across_x(early_other)
     kept, sent, qkv_g, qkv_bg, vector_g = call(
         mixed_back_body, steps,
@@ -1251,7 +1241,7 @@
          rows_spec(256), whole((8, D)), whole((D, 256)), whole((D, 256)), rows_spec(LANES), rows_spec(LANES)],
         [part_spec, part_spec, whole((D, 256)), whole((1, 256)), whole((8, D))],
         [part_shape, part_shape, shaped((D, 256), F32), shaped((1, 256), F32), shaped((8, D), F32)], (), 1,
-    )(here, slot_tokens, one, query_g, key_g, value_g, hidden_g, vectors, qkv_w, expand_w, cos, sin)
+    )(facts, slot_tokens, one, query_g, key_g, value_g, hidden_g, vectors, qkv_w, expand_w, cos, sin)
     in_rows = to_owner(summed(kept, sent))
 
     values = residual.astype(F32)
@@ -1262,21 +1252,18 @@
     late = call(
         late_body, (1,), [whole((D, 256)), whole((8, D)), whole((1, 256))], whole((LATE_ROWS, LANES)),
         shaped((LATE_ROWS, LANES), BF16), [pltpu.VMEM((32, LANES), F32)], 1,
-    )(head_scalar, qkv_g, vector_g, qkv_bg)
+    )(facts, qkv_g, vector_g, qkv_bg)
     late_came = lax.ppermute(late, "x", [(1, 0)])
-    x_scalar = x.astype(jnp.int32).reshape(1)
     sent_g = call(
         both_body, (1,),
         [whole(plane), whole(plane), whole((LATE_ROWS, LANES)), whole((LATE_ROWS, LANES))],
         whole(plane), shaped(plane, BF16), (), 1,
-    )(x_scalar, early, early_came, late, late_came)
+    )(facts, early, early_came, late, late_came)
     got_g = lax.all_to_all(sent_g, RING, 0, 0, tiled=True)
-    begin_g = (chunk - PER * D) * owner - skipped * D + 4 * D
-    scalars_g = jnp.stack([begin_g // LANES, begin_g % LANES, kind, vector_row]).astype(jnp.int32)
     taken = call(
         grads_in_body, (1,), [whole(got_g.shape)], whole((TAKE_ROWS, LANES)), shaped((TAKE_ROWS, LANES), F32),
         [pltpu.VMEM((SHIFT_ROWS, LANES), F32)], 1,
-    )(scalars_g, got_g).reshape(-1)
+    )(facts, got_g).reshape(-1)
     from_before = lax.ppermute(taken[D + chunk : 5 * D + chunk], ALL, onward)
     from_after = lax.ppermute(taken[:D], ALL, backward)
     gradients = (
@@ -1285,7 +1272,7 @@
         + jnp.pad(from_after, (chunk - D, 0))
     )
 
-    outputs = (values + out_rows + (biases[0] + biases[1])).astype(BF16)
+    outputs = (values + out_rows + (vectors[4] + vectors[5])).astype(BF16)
     first_token = ((lax.axis_index("z") * 2 + lax.axis_index("y")) * 4 + x * 2 + lax.axis_index("core")) * span
     token = first_token + jnp.arange(span, dtype=jnp.int32)
     live = token[None, :] < lengths[:, None]

time: 413 us -> 392 us (0.949)
  waiting for transfers between devices: 155 us -> 142 us
    ppermute x1 -> x0, waiting for transfers between devices: 9.64 us -> none  [by_head(): came = lax.ppermute(got[:9], 'x', [(0, 1)])]
    ppermute x6 -> x5, starting transfers between devices: 18.9 us -> 21.8 us  [across_x(): return lax.ppermute(block, 'x', [(0, 1), (1, 0)])]
    pallas_call x3 -> x2, Pallas kernels: 18.9 us -> 16.2 us  [the longest x1 12.4 us: by_head(): call(mixed_body, steps, [token_spec, whole((16, LANES)), whole((8, D)), w...]
    ppermute x6 -> x5, waiting for transfers between devices: 32.6 us -> 31.6 us  [across_x(): return lax.ppermute(block, 'x', [(0, 1), (1, 0)])]
  transfers between devices with their start and end apart: 22 -> 20, of which waited for: 10 -> 8; matrix products, arithmetic and copies ran while one was open for 6% -> 5% of each run, Pallas kernels for 15% -> 15%
where the time goes in v1:
time: 392 us; the launch traced here: 390 us
  waiting for transfers between devices  142 us (36%)
  Pallas kernels  105 us (27%)
  blocking collectives  51.3 us (13%)
  starting transfers between devices  50.5 us (13%)
  other arithmetic  16.9 us (4%)
  between operations  14 us (4%)
  local copies, waits for them, and re-layouts  11.1 us (3%)
    all_to_all x1, blocking collectives, by_head(): got = lax.all_to_all(sent, RING, 0, 0, tiled=True)  51.3 us
    reduce_scatter x1, waiting for transfers between devices, by_head(): lax.psum_scatter(partial_out.reshape(16, 2, span, width), RING, scatter_d...  45.9 us
    ppermute x5, waiting for transfers between devices, across_x(): return lax.ppermute(block, 'x', [(0, 1), (1, 0)])  31.6 us
    ppermute x4, waiting for transfers between devices, summed(): came = lax.ppermute(sent, axis, route)  24.3 us
    ppermute x5, starting transfers between devices, across_x(): return lax.ppermute(block, 'x', [(0, 1), (1, 0)])  21.8 us
    ppermute x1, waiting for transfers between devices, by_head(): late_came = lax.ppermute(late, 'x', [(1, 0)])  19.5 us
    all_to_all x1, waiting for transfers between devices, by_head(): second_g = lax.all_to_all(second_g, RING, 0, 0, tiled=True)  17.9 us
    pallas_call x1, Pallas kernels, by_head(): call(feed_body, steps, [rows_spec(D), rows_spec(HD), token_spec, whole((D...  16.9 us
  transfers between devices with their start and end apart: 20, of which 8 were waited for; matrix products, arithmetic and copies ran while one was open for 5% of the time, Pallas kernels for 15%

profile of v1, /device:TPU:0, one launch (start us, length us, event | category | flops | bytes accessed | tf_op | source)
XLA Modules:
  0.0 390.5 jit_solution(3257669817107775533)
XLA Ops:
  11.4 6.3 %collective-permute-done = bf16[2,64,1024]{2,1,0:T(8,128)(2,1)S(1)} collective-permute-done((bf16[2,64,1024]{2,1,0:T(8,128)(2,1)S(1)}, bf16[2,64,1024]{2,1,0:T(8,128)(2,1)S(1)}, u32[]{:S(2)}, u32[]{:S(2)}) %collective-permute-start) | collective-permute-done | bytes 262176 | tf_op jit(solution)/shard_map/ppermute | solution.py:1076
  20.8 4.5 %collective-permute-start.1 = (f32[1024]{0:T(1024)S(1)}, f32[1024]{0:T(1024)S(1)}, u32[]{:S(2)}, u32[]{:S(2)}) collective-permute-start(f32[1024]{0:T(1024)S(1)} %slice.67), channel_id=1, source_target_pairs={{0,1},{1,2},{2,3},{3,4},{4,5},{5,6},{6,7},{7,8},{8,9},{9,10},{10,1... | collective-permute-start | bytes 12296 | tf_op jit(solution)/shard_map/ppermute | solution.py:1109
  29.9 7.2 %shard_map.118 = bf16[16,240,128]{2,1,0:T(8,128)(2,1)} custom-call(s32[12]{0:T(128)} %stack.92.scalars.facts.lengths.here, f32[8,128]{1,0:T(8,128)} %bitcast.61, f32[3080,128]{1,0:T(8,128)} %pad_bitcast_fusion.own, f32[32,128]{1,0:T(8,128)} %bitcast.55, bf16[16,128]{1,0:T(8,128)(2,1)} %maximum_maximum_fusion.places), custom_call_target="tpu_custom_call" | custom-call | tf_op jit(solution)/shard_map/pallas_call | solution.py:1131
  37.1 51.3 %all_to_all.20.own = bf16[16,240,128]{2,1,0:T(8,128)(2,1)S(1)} all-to-all(bf16[16,240,128]{2,1,0:T(8,128)(2,1)} %shard_map.118), channel_id=1, replica_groups=mesh['x'=2,'core'=2,'z'=4,'y'=2] {'core','z','y'}, dimensions={0} | all-to-all | bytes 1966080 | tf_op jit(solution)/shard_map/all_to_all | solution.py:1139
  89.9 21.9 %collective-permute-done.3.came = bf16[16,240,128]{2,1,0:T(8,128)(2,1)S(1)} collective-permute-done((bf16[16,240,128]{2,1,0:T(8,128)(2,1)S(1)}, bf16[16,240,128]{2,1,0:T(8,128)(2,1)S(1)}, u32[]{:S(2)}, u32[]{:S(2)}) %collective-permute-start.3) | collective-permute-done | bytes 983072 | tf_op jit(solution)/shard_map/ppermute | solution.py:1076
  112.7 3.8 shard_map.119
  116.5 3.8 all-to-all-start.1
  120.9 12.4 %shard_map.120 = (bf16[2048,1024]{1,0:T(8,128)(2,1)}, bf16[2048,1024]{1,0:T(8,128)(2,1)}, bf16[2048,64]{1,0:T(8,128)(2,1)}, bf16[2048,64]{1,0:T(8,128)(2,1)}, bf...) custom-call(bf16[2,8,2,64,1024]{4,3,2,1,0:T(8,128)(2,1)} %bitcast.43, ...), custom_call_target="tpu_custom_call" | custom-call | tf_op jit(solution)/shard_map/pallas_call | solution.py:1183
  133.2 14.7 %shard_map.121 = (bf16[2048,64]{1,0:T(8,128)(2,1)}, f32[64,2048]{1,0:T(8,128)}, f32[1,2048]{1,0:T(1,128)}) custom-call(s32[12]{0:T(128)} %stack.92.scalars.facts.lengths.here, bf16[2048,64]{1,0:T(8,128)(2,1)} %get-tuple-element.55.query, bf16[2048,64]{1,0:T(8,128)(2,1)} %get-tuple-element.56.key, bf16[2048,64]{1,0:T(8,128)(2,1)} %get-tuple-element.57.value), custom_call_target="tpu_custom_call" | custom-call | tf_op jit(solution)/shard_map/pallas_call | solution.py:1189
  153.1 16.9 %shard_map.123 = (bf16[2,8,2,64,1024]{4,3,2,1,0:T(8,128)(2,1)}, bf16[2048,64]{1,0:T(8,128)(2,1)}, bf16[2048,256]{1,0:T(8,128)(2,1)}, f32[256,1024]{1,0:T(8,128)}...) custom-call(s32[12]{0:T(128)} %stack.92.scalars.facts.lengths.here, ...), custom_call_target="tpu_custom_call" | custom-call | tf_op jit(solution)/shard_map/pallas_call | solution.py:1202
  172.4 12.3 %shard_map.125 = (bf16[2048,64]{1,0:T(8,128)(2,1)}, bf16[2048,64]{1,0:T(8,128)(2,1)}, bf16[2048,64]{1,0:T(8,128)(2,1)}) custom-call(s32[12]{0:T(128)} %stack.92.scalars.facts.lengths.here, bf16[2048,64]{1,0:T(8,128)(2,1)} %get-tuple-element.55.query, bf16[2048,64]{1,0:T(8,128)(2,1)} %get-tuple-element.56.key, bf16[2048,64]{1,0:T(8,128)(2,1)} %get-tuple-element.57.value, ...), custom_call_target="tpu_custom_call" | custom-call | tf_op jit(solution)/shard_map/pallas_call | solution.py:1220
  184.7 13.7 %shard_map.126 = (bf16[8,2,64,1024]{3,2,1,0:T(8,128)(2,1)}, bf16[8,2,64,1024]{3,2,1,0:T(8,128)(2,1)}, f32[1024,256]{1,0:T(8,128)}, f32[1,256]{1,0:T(1,128)}, f32[8,1024]{1,0:T(8,128)}) custom-call(s32[12]{0:T(128)} %stack.92.scalars.facts.lengths.here, bf16[2,8,2,64,1024]{4,3,2,1,0:T(8,128)(2,1)} %bitcast.44, bf16[2048,1024]{1,0:T(8,128)(2,1)} %get-tuple-element.67.one, ...), custom_call_target="tpu_custom_call" | custom-call | tf_op jit(solution)/shard_map/pallas_call | solution.py:1238
  198.5 3.8 all-to-all-start.2
  202.9 17.9 %all-to-all-done.2.second = bf16[16,160,128]{2,1,0:T(8,128)(2,1)S(1)} async-done(((bf16[16,160,128]{2,1,0:T(8,128)(2,1)}), bf16[16,160,128]{2,1,0:T(8,128)(2,1)S(1)}, u32[]{:S(2)}, u32[]{:S(2)}) %all-to-all-start.2) | async-done | bytes 655392 | tf_op jit(solution)/shard_map/all_to_all | solution.py:1215
  221.7 4.7 %shard_map.127 = (bf16[16,224,128]{2,1,0:T(8,128)(2,1)}, bf16[16,224,128]{2,1,0:T(8,128)(2,1)}) custom-call(s32[12]{0:T(128)} %stack.92.scalars.facts.lengths.here, bf16[16,160,128]{2,1,0:T(8,128)(2,1)} %copy-done.5, f32[1024,256]{1,0:T(8,128)} %get-tuple-element.84.expand_g, f32[1,1024]{1,0:T(1,128)} %broadcast_select_fusion.bias_g, ...), custom_call_target="tpu_custom_call" | custom-call | tf_op jit(solution)/shard_map/pallas_call | solution.py:1230
  226.3 10.6 %collective-permute-start.10 = (bf16[16,224,128]{2,1,0:T(8,128)(2,1)}, bf16[16,224,128]{2,1,0:T(8,128)(2,1)S(1)}, u32[]{:S(2)}, u32[]{:S(2)}) collective-permute-start(bf16[16,224,128]{2,1,0:T(8,128)(2,1)} %get-tuple-element.88), channel_id=1, source_target_pairs={{0,16},{16,0},{1,17},{17,1},{2,18},{18,2},{3,19},{19,3},{4,20},{20... | collective-permute-start | bytes 2752520 | tf_op jit(solution)/shard_map/ppermute | solution.py:1076
  236.9 4.2 %add_convert_fusion.1 = (bf16[4,2,64,1024]{3,2,1,0:T(8,128)(2,1)S(1)}, bf16[4,2,64,1024]{3,2,1,0:T(8,128)(2,1)}) fusion(bf16[8,2,64,1024]{3,2,1,0:T(8,128)(2,1)} %collective-permute-done.5, bf16[8,2,64,1024]{3,2,1,0:T(8,128)(2,1)} %get-tuple-element.80), kind=kLoop, calls=%fused_computation.1 | loop fusion | flops 4194304 | bytes 6291456 | tf_op jit(solution)/shard_map/convert_element_type | solution.py:1167
  245.7 19.5 %collective-permute-done.11.late_came = bf16[1600,128]{1,0:T(8,128)(2,1)S(1)} collective-permute-done((bf16[1600,128]{1,0:T(8,128)(2,1)}, bf16[1600,128]{1,0:T(8,128)(2,1)S(1)}, u32[]{:S(2)}, u32[]{:S(2)}) %collective-permute-start.11) | collective-permute-done | bytes 409632 | tf_op jit(solution)/shard_map/ppermute | solution.py:1256
  269.9 4.5 %all-to-all-start.3 = ((bf16[16,224,128]{2,1,0:T(8,128)(2,1)}), bf16[16,224,128]{2,1,0:T(8,128)(2,1)}, u32[]{:S(2)}, u32[]{:S(2)}) async-start(bf16[16,224,128]{2,1,0:T(8,128)(2,1)} %shard_map.129), calls=%async_computation.4 | async-start | bytes 1835008 | tf_op jit(solution)/shard_map/all_to_all | solution.py:1262
  279.0 24.3 %collective-permute-done.7 = bf16[2,2,64,1024]{3,2,1,0:T(8,128)(2,1)S(1)} collective-permute-done((bf16[2,2,64,1024]{3,2,1,0:T(8,128)(2,1)}, bf16[2,2,64,1024]{3,2,1,0:T(8,128)(2,1)S(1)}, u32[]{:S(2)}, u32[]{:S(2)}) %collective-permute-start.7) | collective-permute-done | bytes 524320 | tf_op jit(solution)/shard_map/ppermute | solution.py:1162
  306.7 7.9 %shard_map.130 = f32[3120,128]{1,0:T(8,128)} custom-call(s32[12]{0:T(128)} %stack.92.scalars.facts.lengths.here, bf16[16,224,128]{2,1,0:T(8,128)(2,1)} %all-to-all-done.3.got), custom_call_target="tpu_custom_call" | custom-call | tf_op jit(solution)/shard_map/pallas_call | solution.py:1263
  321.1 5.1 %collective-permute-start.9 = (bf16[64,1024]{1,0:T(8,128)(2,1)S(1)}, bf16[64,1024]{1,0:T(8,128)(2,1)S(1)}, u32[]{:S(2)}, u32[]{:S(2)}) collective-permute-start(bf16[64,1024]{1,0:T(8,128)(2,1)S(1)} %get-tuple-element.108), channel_id=1, source_target_pairs={{0,16},{16,0},{1,17},{17,1},{2,18},{18,2},{3,19},{19,3},{4,20},{20... | collective-permute-start | bytes 393224 | tf_op jit(solution)/shard_map/ppermute | solution.py:1076
  326.2 4.4 %add_multiply_fusion = (f32[393632]{0:T(1024)}, f32[393632]{0:T(1024)}, f32[393632]{0:T(1024)}, f32[393632]{0:T(1024)}) fusion(f32[393632]{0:T(1024)S(1)} %copy-done.6, f32[393632]{0:T(1024)S(1)} %copy-done.1, f32[393632]{0:T(1024)} %param.12, f32[1024]{0:T(1024)S(1)} %collective-permute-done.13, f32[4096]{0:T(1024)S(1)} %collective-permute-done.12, ...), kind=kLoop, calls=%fused_computation.4 | loop fusion | flops 3936320 | bytes 12616704 | tf_op jit(solution)/shard_map/add | solution.py:1288
  330.9 45.9 %reduce-scatter.2.cloned.1.call-done = bf16[1,2,64,1024]{3,2,1,0:T(8,128)(2,1)} async-done(((bf16[16,2,64,1024]{3,2,1,0:T(8,128)(2,1)}), bf16[1,2,64,1024]{3,2,1,0:T(8,128)(2,1)}) %reduce-scatter.2.cloned.1.call-update) | async-done | bytes 262160 | tf_op jit(solution)/shard_map/reduce_scatter | solution.py:1216
  (99 shorter events, 55.0 us)
Async XLA Ops:
  7.2 113.7 %all-gather.5.cloned.1.call-start = ((), (), s32[]{:S(2)}) async-start(), calls=%async_computation.6 | async-start | bytes 4456448 | tf_op jit(solution)/shard_map/all_gather | solution.py:1099
  8.4 9.3 %collective-permute-start = (bf16[2,64,1024]{2,1,0:T(8,128)(2,1)S(1)}, bf16[2,64,1024]{2,1,0:T(8,128)(2,1)S(1)}, u32[]{:S(2)}, u32[]{:S(2)}) collective-permute-start(bf16[2,64,1024]{2,1,0:T(8,128)(2,1)S(1)} %get-tuple-element.105), channel_id=1, source_target_pairs={{0,16},{16,0},{1,17},{17,1},{2,18},{18,2},{3,19},{19,3},{4,20},{20... | collective-permute-start | bytes 786440 | tf_op jit(solution)/shard_map/ppermute | solution.py:1076
  18.7 134.4 %all-gather.7.cloned.1.call-start = ((), (), s32[]{:S(2)}) async-start(), calls=%async_computation.7 | async-start | bytes 4456448 | tf_op jit(solution)/shard_map/all_gather | solution.py:1100
  19.4 9.9 %collective-permute-start.2 = (f32[4096]{0:T(1024)S(1)}, f32[4096]{0:T(1024)S(1)}, u32[]{:S(2)}, u32[]{:S(2)}) collective-permute-start(f32[4096]{0:T(1024)S(1)} %slice.68), channel_id=1, source_target_pairs={{1,0},{2,1},{3,2},{4,3},{5,4},{6,5},{7,6},{8,7},{9,8},{10,9},{11,1... | collective-permute-start | bytes 49160 | tf_op jit(solution)/shard_map/ppermute | solution.py:1110
  20.8 8.5 %collective-permute-start.1 = (f32[1024]{0:T(1024)S(1)}, f32[1024]{0:T(1024)S(1)}, u32[]{:S(2)}, u32[]{:S(2)}) collective-permute-start(f32[1024]{0:T(1024)S(1)} %slice.67), channel_id=1, source_target_pairs={{0,1},{1,2},{2,3},{3,4},{4,5},{5,6},{6,7},{7,8},{8,9},{9,10},{10,1... | collective-permute-start | bytes 12296 | tf_op jit(solution)/shard_map/ppermute | solution.py:1109
  88.4 23.3 %copy-start.3 = (bf16[16,240,128]{2,1,0:T(8,128)(2,1)}, bf16[16,240,128]{2,1,0:T(8,128)(2,1)S(1)}, u32[]{:S(2)}) copy-start(bf16[16,240,128]{2,1,0:T(8,128)(2,1)S(1)} %all_to_all.20.own) | copy-start | bytes 2949124
  88.4 23.3 %collective-permute-start.3 = (bf16[16,240,128]{2,1,0:T(8,128)(2,1)S(1)}, bf16[16,240,128]{2,1,0:T(8,128)(2,1)S(1)}, u32[]{:S(2)}, u32[]{:S(2)}) collective-permute-start(bf16[16,240,128]{2,1,0:T(8,128)(2,1)S(1)} %all_to_all.20.own), channel_id=1, source_target_pairs={{0,16},{16,0},{1,17},{17,1},{2,18},{18,2},{3,19},{19,3},{4,20},{20... | collective-permute-start | bytes 2949128 | tf_op jit(solution)/shard_map/ppermute | solution.py:1076
  116.5 33.5 %all-to-all-start.1 = ((bf16[16,160,128]{2,1,0:T(8,128)(2,1)}), bf16[16,160,128]{2,1,0:T(8,128)(2,1)S(1)}, u32[]{:S(2)}, u32[]{:S(2)}) async-start(bf16[16,160,128]{2,1,0:T(8,128)(2,1)} %get-tuple-element.54), calls=%async_computation.1 | async-start | bytes 1310720 | tf_op jit(solution)/shard_map/all_to_all | solution.py:1150
  184.7 17.7 %copy-start.13 = (f32[1,1024]{1,0:T(1,128)S(1)}, f32[1,1024]{1,0:T(1,128)}, u32[]{:S(2)}) copy-start(f32[1,1024]{1,0:T(1,128)} %get-tuple-element.85) | copy-start | bytes 12292
  198.4 38.5 %collective-permute-start.5 = (bf16[8,2,64,1024]{3,2,1,0:T(8,128)(2,1)}, bf16[8,2,64,1024]{3,2,1,0:T(8,128)(2,1)}, u32[]{:S(2)}, u32[]{:S(2)}) collective-permute-start(bf16[8,2,64,1024]{3,2,1,0:T(8,128)(2,1)} %get-tuple-element.81), channel_id=1, source_target_pairs={{0,8},{8,0},{1,9},{9,1},{2,10},{10,2},{3,11},{11,3},{4,12},{12,4},... | collective-permute-start | bytes 6291464 | tf_op jit(solution)/shard_map/ppermute | solution.py:1162
  198.5 22.3 %all-to-all-start.2 = ((bf16[16,160,128]{2,1,0:T(8,128)(2,1)}), bf16[16,160,128]{2,1,0:T(8,128)(2,1)S(1)}, u32[]{:S(2)}, u32[]{:S(2)}) async-start(bf16[16,160,128]{2,1,0:T(8,128)(2,1)} %shard_map.124), calls=%async_computation.3 | async-start | bytes 1310720 | tf_op jit(solution)/shard_map/all_to_all | solution.py:1215
  226.3 38.9 %collective-permute-start.10 = (bf16[16,224,128]{2,1,0:T(8,128)(2,1)}, bf16[16,224,128]{2,1,0:T(8,128)(2,1)S(1)}, u32[]{:S(2)}, u32[]{:S(2)}) collective-permute-start(bf16[16,224,128]{2,1,0:T(8,128)(2,1)} %get-tuple-element.88), channel_id=1, source_target_pairs={{0,16},{16,0},{1,17},{17,1},{2,18},{18,2},{3,19},{19,3},{4,20},{20... | collective-permute-start | bytes 2752520 | tf_op jit(solution)/shard_map/ppermute | solution.py:1076
  241.1 33.7 %collective-permute-start.6 = (bf16[4,2,64,1024]{3,2,1,0:T(8,128)(2,1)}, bf16[4,2,64,1024]{3,2,1,0:T(8,128)(2,1)}, u32[]{:S(2)}, u32[]{:S(2)}) collective-permute-start(bf16[4,2,64,1024]{3,2,1,0:T(8,128)(2,1)} %get-tuple-element.99), channel_id=1, source_target_pairs={{0,1},{1,0},{2,3},{3,2},{4,5},{5,4},{6,7},{7,6},{8,9},{9,8},{10,11... | collective-permute-start | bytes 3145736 | tf_op jit(solution)/shard_map/ppermute | solution.py:1162
  244.4 20.8 %collective-permute-start.11 = (bf16[1600,128]{1,0:T(8,128)(2,1)}, bf16[1600,128]{1,0:T(8,128)(2,1)S(1)}, u32[]{:S(2)}, u32[]{:S(2)}) collective-permute-start(bf16[1600,128]{1,0:T(8,128)(2,1)} %shard_map.128.late), channel_id=1, source_target_pairs={{16,0},{17,1},{18,2},{19,3},{20,4},{21,5},{22,6},{23,7},{24,8},{25... | collective-permute-start | bytes 1228808 | tf_op jit(solution)/shard_map/ppermute | solution.py:1256
  269.9 36.8 %all-to-all-start.3 = ((bf16[16,224,128]{2,1,0:T(8,128)(2,1)}), bf16[16,224,128]{2,1,0:T(8,128)(2,1)}, u32[]{:S(2)}, u32[]{:S(2)}) async-start(bf16[16,224,128]{2,1,0:T(8,128)(2,1)} %shard_map.129), calls=%async_computation.4 | async-start | bytes 1835008 | tf_op jit(solution)/shard_map/all_to_all | solution.py:1262
  274.4 102.4 %reduce-scatter.2.cloned.1.call-start = ((), (), s32[]{:S(2)}) async-start(), calls=%async_computation.5 | async-start | bytes 4456448 | tf_op jit(solution)/shard_map/reduce_scatter | solution.py:1216
  277.2 26.1 %collective-permute-start.7 = (bf16[2,2,64,1024]{3,2,1,0:T(8,128)(2,1)}, bf16[2,2,64,1024]{3,2,1,0:T(8,128)(2,1)S(1)}, u32[]{:S(2)}, u32[]{:S(2)}) collective-permute-start(bf16[2,2,64,1024]{3,2,1,0:T(8,128)(2,1)} %get-tuple-element.101), channel_id=1, source_target_pairs={{0,2},{2,0},{4,6},{6,4},{1,3},{3,1},{5,7},{7,5},{8,10},{10,8},{12,... | collective-permute-start | bytes 1572872 | tf_op jit(solution)/shard_map/ppermute | solution.py:1162
  303.4 17.5 %collective-permute-start.8 = (bf16[1,2,64,1024]{3,2,1,0:T(8,128)(2,1)S(1)}, bf16[1,2,64,1024]{3,2,1,0:T(8,128)(2,1)S(1)}, u32[]{:S(2)}, u32[]{:S(2)}) collective-permute-start(bf16[1,2,64,1024]{3,2,1,0:T(8,128)(2,1)S(1)} %add_convert_fusion.5), channel_id=1, source_target_pairs={{0,4},{4,0},{2,6},{6,2},{1,5},{5,1},{3,7},{7,3},{8,12},{12,8},{10,... | collective-permute-start | bytes 786440 | tf_op jit(solution)/shard_map/ppermute | solution.py:1162
  306.7 19.5 %copy-start.6 = (f32[393632]{0:T(1024)S(1)}, f32[393632]{0:T(1024)}, u32[]{:S(2)}) copy-start(f32[393632]{0:T(1024)} %param.13) | copy-start | bytes 4723588
  315.6 10.6 %collective-permute-start.12 = (f32[4096]{0:T(1024)S(1)}, f32[4096]{0:T(1024)S(1)}, u32[]{:S(2)}, u32[]{:S(2)}) collective-permute-start(f32[4096]{0:T(1024)S(1)} %slice.101), channel_id=1, source_target_pairs={{0,1},{1,2},{2,3},{3,4},{4,5},{5,6},{6,7},{7,8},{8,9},{9,10},{10,1... | collective-permute-start | bytes 49160 | tf_op jit(solution)/shard_map/ppermute | solution.py:1267
  319.7 6.6 %collective-permute-start.13 = (f32[1024]{0:T(1024)S(1)}, f32[1024]{0:T(1024)S(1)}, u32[]{:S(2)}, u32[]{:S(2)}) collective-permute-start(f32[1024]{0:T(1024)S(1)} %slice_bitcast_fusion), channel_id=1, source_target_pairs={{1,0},{2,1},{3,2},{4,3},{5,4},{6,5},{7,6},{8,7},{9,8},{10,9},{11,1... | collective-permute-start | bytes 12296 | tf_op jit(solution)/shard_map/ppermute | solution.py:1268
  321.1 61.7 %copy-start.7 = (bf16[2,64,1024]{2,1,0:T(8,128)(2,1)S(1)}, bf16[2,64,1024]{2,1,0:T(8,128)(2,1)}, u32[]{:S(2)}) copy-start(bf16[2,64,1024]{2,1,0:T(8,128)(2,1)} %param.8) | copy-start | bytes 786436
  321.1 9.5 %collective-permute-start.9 = (bf16[64,1024]{1,0:T(8,128)(2,1)S(1)}, bf16[64,1024]{1,0:T(8,128)(2,1)S(1)}, u32[]{:S(2)}, u32[]{:S(2)}) collective-permute-start(bf16[64,1024]{1,0:T(8,128)(2,1)S(1)} %get-tuple-element.108), channel_id=1, source_target_pairs={{0,16},{16,0},{1,17},{17,1},{2,18},{18,2},{3,19},{19,3},{4,20},{20... | collective-permute-start | bytes 393224 | tf_op jit(solution)/shard_map/ppermute | solution.py:1076
  377.8 5.0 %collective-permute-start.4 = (bf16[64,1024]{1,0:T(8,128)(2,1)S(1)}, bf16[64,1024]{1,0:T(8,128)(2,1)S(1)}, u32[]{:S(2)}, u32[]{:S(2)}) collective-permute-start(bf16[64,1024]{1,0:T(8,128)(2,1)S(1)} %get-tuple-element.111), channel_id=1, source_target_pairs={{0,16},{16,0},{1,17},{17,1},{2,18},{18,2},{3,19},{19,3},{4,20},{20... | collective-permute-start | bytes 393224 | tf_op jit(solution)/shard_map/ppermute | solution.py:1076
  (12 other events, 51.6 us)
Sparse Core Ops, SparseCore 0:
  18.8 68.9 all-gather.4
  90.5 59.8 all-gather.6
  306.8 69.9 reduce-scatter.1

commit v2 on v1

--- a/solution.py
+++ b/solution.py
@@ -1005,38 +1005,41 @@
         value_g[...] = value_sum[...].astype(BF16)
 
 
-def feed_body(
-    here, two, attended, cotangent, expand_w, expand_b, shrink_w, dense_w,
-    partial_out, attended_g, hidden_g, shrink_g, dense_g, expand_g, expand_bg, bias_g,
-):
-    at = pl.program_id(0)
-
-    @pl.when(at == 0)
-    def _():
-        for total in (shrink_g, dense_g, expand_g, expand_bg, bias_g):
-            total[...] = jnp.zeros(total.shape, F32)
-
-    normed, mixed = two[...], attended[...]
-    hidden = mm(normed, expand_w[...]) + expand_b[...]
+def feed_body(two, attended, expand_w, expand_b, shrink_w, dense_w, partial_out, active_out, slope_out):
+    hidden = mm(two[...], expand_w[...]) + expand_b[...]
     error = lax.erf(hidden * math.sqrt(0.5))
     cumulative = 0.5 * (1.0 + error)
     active = (hidden * cumulative).astype(BF16)
-    partial = mm(mixed, dense_w[...]) + mm(active, shrink_w[...])
+    active_out[...] = active
+    slope_out[...] = cumulative + hidden * jnp.exp(-0.5 * hidden * hidden) * (1.0 / math.sqrt(2.0 * math.pi))
+    partial = mm(attended[...], dense_w[...]) + mm(active, shrink_w[...])
     step = BLOCK // 4
     for i, (core, x) in enumerate(((0, 0), (1, 0), (0, 1), (1, 1))):
         partial_out[core, 0, x] = partial[step * i : step * i + step].astype(BF16)
+
+
+def feed_back_body(
+    here, two, attended, cotangent, active, slope, shrink_w, dense_w,
+    attended_g, hidden_g, shrink_g, dense_g, expand_g, expand_bg, bias_g,
+):
+    at = pl.program_id(0)
+
+    @pl.when(at == 0)
+    def _():
+        for total in (shrink_g, dense_g, expand_g, expand_bg, bias_g):
+            total[...] = jnp.zeros(total.shape, F32)
+
     token = at * BLOCK + lax.broadcasted_iota(jnp.int32, (BLOCK, D), 0)
     seed = jnp.where(token < here[LENGTH], token_rows(cotangent).astype(F32), 0.0)
     bias_g[...] += jnp.sum(seed, axis=0, keepdims=True)
     seed = seed.astype(BF16)
     attended_g[...] = mm(seed, dense_w[...], ((1,), (1,))).astype(BF16)
-    slope = cumulative + hidden * jnp.exp(-0.5 * hidden * hidden) * (1.0 / math.sqrt(2.0 * math.pi))
-    back = (mm(seed, shrink_w[...], ((1,), (1,))) * slope).astype(BF16)
+    back = (mm(seed, shrink_w[...], ((1,), (1,))) * slope[...]).astype(BF16)
     hidden_g[...] = back
     expand_bg[...] += jnp.sum(back.astype(F32), axis=0, keepdims=True)
-    shrink_g[...] += mm(active, seed, ((0,), (0,)))
-    dense_g[...] += mm(mixed, seed, ((0,), (0,)))
-    expand_g[...] += mm(normed, back, ((0,), (0,)))
+    shrink_g[...] += mm(active[...], seed, ((0,), (0,)))
+    dense_g[...] += mm(attended[...], seed, ((0,), (0,)))
+    expand_g[...] += mm(two[...], back, ((0,), (0,)))
 
 
 def mixed_back_body(
@@ -1199,24 +1202,30 @@
         [shaped((HD, D), BF16), shaped((256, D), BF16)],
     )(second)
 
-    partial_out, attended_g, hidden_g, shrink_g, dense_g, expand_g, expand_bg, bias_g = call(
+    partial_out, active, slope = call(
         feed_body, steps,
-        [rows_spec(D), rows_spec(HD), token_spec, whole((D, 256)), whole((1, 256)), whole((256, D)), whole((HD, D))],
-        [token_spec, rows_spec(HD), rows_spec(256), whole((256, D)), whole((HD, D)), whole((D, 256)),
-         whole((1, 256)), whole((1, D))],
-        [shaped(tokens_shape, BF16), narrow, shaped((count, 256), BF16), shaped((256, D), F32), shaped((HD, D), F32),
+        [rows_spec(D), rows_spec(HD), whole((D, 256)), whole((1, 256)), whole((256, D)), whole((HD, D))],
+        [token_spec, rows_spec(256), rows_spec(256)],
+        [shaped(tokens_shape, BF16), shaped((count, 256), BF16), shaped((count, 256), F32)],
+    )(two, attended, expand_w, expand_b, shrink_w, dense_w)
+    out_rows = lax.psum_scatter(
+        partial_out.reshape(16, 2, span, width), RING, scatter_dimension=0, tiled=True
+    )[0]
+    out_rows = to_owner(out_rows)
+    attended_g, hidden_g, shrink_g, dense_g, expand_g, expand_bg, bias_g = call(
+        feed_back_body, steps,
+        [rows_spec(D), rows_spec(HD), token_spec, rows_spec(256), rows_spec(256), whole((256, D)), whole((HD, D))],
+        [rows_spec(HD), rows_spec(256), whole((256, D)), whole((HD, D)), whole((D, 256)), whole((1, 256)),
+         whole((1, D))],
+        [narrow, shaped((count, 256), BF16), shaped((256, D), F32), shaped((HD, D), F32),
          shaped((D, 256), F32), shaped((1, 256), F32), shaped((1, D), F32)], (), 1,
-    )(facts, two, attended, slot_cotangent, expand_w, expand_b, shrink_w, dense_w)
+    )(facts, two, attended, slot_cotangent, active, slope, shrink_w, dense_w)
     second_g = call(
         rows_out_body, (1,), [whole((HD, D)), whole((256, D))], whole((16, 160, LANES)),
         shaped((16, 160, LANES), BF16),
     )(dense_g, shrink_g)
     attended_g, second_g = lax.optimization_barrier((attended_g, second_g))
     second_g = lax.all_to_all(second_g, RING, 0, 0, tiled=True)
-    out_rows = lax.psum_scatter(
-        partial_out.reshape(16, 2, span, width), RING, scatter_dimension=0, tiled=True
-    )[0]
-    out_rows = to_owner(out_rows)
     query_g, key_g, value_g = call(
         attend_back_body, steps,
         [rows_spec(HD), whole((count, HD)), whole((count, HD)), rows_spec(HD), columns_spec(HD), columns_spec(1)],

time: 392 us -> 399 us (1.018)
  Pallas kernels: 105 us -> 111 us
    pallas_call x1 -> x2, Pallas kernels: 16.9 us -> 23.5 us  [the longest x1 12.1 us: by_head(): call(feed_back_body, steps, [rows_spec(D), rows_spec(HD), token_spec, row...]
  transfers between devices with their start and end apart: 20 -> 20, of which waited for: 8 -> 8; matrix products, arithmetic and copies ran while one was open for 5% -> 5% of each run, Pallas kernels for 15% -> 18%
where the time goes in v2:
time: 399 us; the launch traced here: 397 us
  waiting for transfers between devices  142 us (36%)
  Pallas kernels  111 us (28%)
  blocking collectives  51.2 us (13%)
  starting transfers between devices  50.5 us (13%)
  other arithmetic  16.9 us (4%)
  between operations  14 us (4%)
  local copies, waits for them, and re-layouts  11.1 us (3%)
    all_to_all x1, blocking collectives, by_head(): got = lax.all_to_all(sent, RING, 0, 0, tiled=True)  51.2 us
    reduce_scatter x1, waiting for transfers between devices, by_head(): lax.psum_scatter(partial_out.reshape(16, 2, span, width), RING, scatter_d...  45.9 us
    ppermute x5, waiting for transfers between devices, across_x(): return lax.ppermute(block, 'x', [(0, 1), (1, 0)])  31.7 us
    ppermute x4, waiting for transfers between devices, summed(): came = lax.ppermute(sent, axis, route)  24.3 us
    ppermute x5, starting transfers between devices, across_x(): return lax.ppermute(block, 'x', [(0, 1), (1, 0)])  21.8 us
    ppermute x1, waiting for transfers between devices, by_head(): late_came = lax.ppermute(late, 'x', [(1, 0)])  19.5 us
    all_to_all x1, waiting for transfers between devices, by_head(): second_g = lax.all_to_all(second_g, RING, 0, 0, tiled=True)  17.9 us
    pallas_call x1, Pallas kernels, by_head(): call(attend_body, steps, [rows_spec(HD), whole((count, HD)), whole((count...  14.7 us
  transfers between devices with their start and end apart: 20, of which 8 were waited for; matrix products, arithmetic and copies ran while one was open for 5% of the time, Pallas kernels for 18%

profile of v2, /device:TPU:0, one launch (start us, length us, event | category | flops | bytes accessed | tf_op | source)
XLA Modules:
  0.0 397.2 jit_solution(16066984226496444942)
XLA Ops:
  11.4 6.3 %collective-permute-done = bf16[2,64,1024]{2,1,0:T(8,128)(2,1)S(1)} collective-permute-done((bf16[2,64,1024]{2,1,0:T(8,128)(2,1)S(1)}, bf16[2,64,1024]{2,1,0:T(8,128)(2,1)S(1)}, u32[]{:S(2)}, u32[]{:S(2)}) %collective-permute-start) | collective-permute-done | bytes 262176 | tf_op jit(solution)/shard_map/ppermute | solution.py:1079
  20.8 4.5 %collective-permute-start.1 = (f32[1024]{0:T(1024)S(1)}, f32[1024]{0:T(1024)S(1)}, u32[]{:S(2)}, u32[]{:S(2)}) collective-permute-start(f32[1024]{0:T(1024)S(1)} %slice.67), channel_id=1, source_target_pairs={{0,1},{1,2},{2,3},{3,4},{4,5},{5,6},{6,7},{7,8},{8,9},{9,10},{10,1... | collective-permute-start | bytes 12296 | tf_op jit(solution)/shard_map/ppermute | solution.py:1112
  30.0 7.2 %shard_map.118 = bf16[16,240,128]{2,1,0:T(8,128)(2,1)} custom-call(s32[12]{0:T(128)} %stack.98.scalars.facts.lengths.here, f32[8,128]{1,0:T(8,128)} %bitcast.61, f32[3080,128]{1,0:T(8,128)} %pad_bitcast_fusion.own, f32[32,128]{1,0:T(8,128)} %bitcast.55, bf16[16,128]{1,0:T(8,128)(2,1)} %maximum_maximum_fusion.places), custom_call_target="tpu_custom_call" | custom-call | tf_op jit(solution)/shard_map/pallas_call | solution.py:1134
  37.2 51.2 %all_to_all.20.own = bf16[16,240,128]{2,1,0:T(8,128)(2,1)S(1)} all-to-all(bf16[16,240,128]{2,1,0:T(8,128)(2,1)} %shard_map.118), channel_id=1, replica_groups=mesh['x'=2,'core'=2,'z'=4,'y'=2] {'core','z','y'}, dimensions={0} | all-to-all | bytes 1966080 | tf_op jit(solution)/shard_map/all_to_all | solution.py:1142
  89.9 21.9 %collective-permute-done.3.came = bf16[16,240,128]{2,1,0:T(8,128)(2,1)S(1)} collective-permute-done((bf16[16,240,128]{2,1,0:T(8,128)(2,1)S(1)}, bf16[16,240,128]{2,1,0:T(8,128)(2,1)S(1)}, u32[]{:S(2)}, u32[]{:S(2)}) %collective-permute-start.3) | collective-permute-done | bytes 983072 | tf_op jit(solution)/shard_map/ppermute | solution.py:1079
  112.8 3.8 shard_map.119
  121.0 12.4 %shard_map.120 = (bf16[2048,1024]{1,0:T(8,128)(2,1)}, bf16[2048,1024]{1,0:T(8,128)(2,1)}, bf16[2048,64]{1,0:T(8,128)(2,1)}, bf16[2048,64]{1,0:T(8,128)(2,1)}, bf...) custom-call(bf16[2,8,2,64,1024]{4,3,2,1,0:T(8,128)(2,1)} %bitcast.43, ...), custom_call_target="tpu_custom_call" | custom-call | tf_op jit(solution)/shard_map/pallas_call | solution.py:1186
  133.4 14.7 %shard_map.121 = (bf16[2048,64]{1,0:T(8,128)(2,1)}, f32[64,2048]{1,0:T(8,128)}, f32[1,2048]{1,0:T(1,128)}) custom-call(s32[12]{0:T(128)} %stack.98.scalars.facts.lengths.here, bf16[2048,64]{1,0:T(8,128)(2,1)} %get-tuple-element.57.query, bf16[2048,64]{1,0:T(8,128)(2,1)} %get-tuple-element.58.key, bf16[2048,64]{1,0:T(8,128)(2,1)} %get-tuple-element.59.value), custom_call_target="tpu_custom_call" | custom-call | tf_op jit(solution)/shard_map/pallas_call | solution.py:1192
  153.1 11.5 %shard_map.123 = (bf16[2,8,2,64,1024]{4,3,2,1,0:T(8,128)(2,1)}, bf16[2048,256]{1,0:T(8,128)(2,1)}, f32[2048,256]{1,0:T(8,128)}) custom-call(bf16[2048,1024]{1,0:T(8,128)(2,1)} %get-tuple-element.55.two, bf16[2048,64]{1,0:T(8,128)(2,1)} %get-tuple-element.61.attended, bf16[1024,256]{1,0:T(8,128)(2,1)} %get-tuple-element.62.expand_w, ...), custom_call_target="tpu_custom_call" | custom-call | tf_op jit(solution)/shard_map/pallas_call | solution.py:1205
  164.6 12.1 %shard_map.124 = (bf16[2048,64]{1,0:T(8,128)(2,1)}, bf16[2048,256]{1,0:T(8,128)(2,1)}, f32[256,1024]{1,0:T(8,128)}, f32[64,1024]{1,0:T(8,128)}, f32[1024,256]{1,...) custom-call(s32[12]{0:T(128)} %stack.98.scalars.facts.lengths.here, bf16[2048,1024]{1,0:T(8,128)(2,1)} %get-tuple-element.55.two, ...), custom_call_target="tpu_custom_call" | custom-call | tf_op jit(solution)/shard_map/pallas_call | solution.py:1215
  179.1 12.3 %shard_map.126 = (bf16[2048,64]{1,0:T(8,128)(2,1)}, bf16[2048,64]{1,0:T(8,128)(2,1)}, bf16[2048,64]{1,0:T(8,128)(2,1)}) custom-call(s32[12]{0:T(128)} %stack.98.scalars.facts.lengths.here, bf16[2048,64]{1,0:T(8,128)(2,1)} %get-tuple-element.57.query, bf16[2048,64]{1,0:T(8,128)(2,1)} %get-tuple-element.58.key, bf16[2048,64]{1,0:T(8,128)(2,1)} %get-tuple-element.59.value, ...), custom_call_target="tpu_custom_call" | custom-call | tf_op jit(solution)/shard_map/pallas_call | solution.py:1229
  191.4 13.7 %shard_map.127 = (bf16[8,2,64,1024]{3,2,1,0:T(8,128)(2,1)}, bf16[8,2,64,1024]{3,2,1,0:T(8,128)(2,1)}, f32[1024,256]{1,0:T(8,128)}, f32[1,256]{1,0:T(1,128)}, f32[8,1024]{1,0:T(8,128)}) custom-call(s32[12]{0:T(128)} %stack.98.scalars.facts.lengths.here, bf16[2,8,2,64,1024]{4,3,2,1,0:T(8,128)(2,1)} %bitcast.44, bf16[2048,1024]{1,0:T(8,128)(2,1)} %get-tuple-element.69.one, ...), custom_call_target="tpu_custom_call" | custom-call | tf_op jit(solution)/shard_map/pallas_call | solution.py:1247
  205.3 3.8 all-to-all-start.2
  209.7 17.9 %all-to-all-done.2.second = bf16[16,160,128]{2,1,0:T(8,128)(2,1)S(1)} async-done(((bf16[16,160,128]{2,1,0:T(8,128)(2,1)}), bf16[16,160,128]{2,1,0:T(8,128)(2,1)S(1)}, u32[]{:S(2)}, u32[]{:S(2)}) %all-to-all-start.2) | async-done | bytes 655392 | tf_op jit(solution)/shard_map/all_to_all | solution.py:1228
  228.4 4.7 %shard_map.128 = (bf16[16,224,128]{2,1,0:T(8,128)(2,1)}, bf16[16,224,128]{2,1,0:T(8,128)(2,1)}) custom-call(s32[12]{0:T(128)} %stack.98.scalars.facts.lengths.here, bf16[16,160,128]{2,1,0:T(8,128)(2,1)} %copy-done.5, f32[1024,256]{1,0:T(8,128)} %get-tuple-element.88.expand_g, f32[1,1024]{1,0:T(1,128)} %broadcast_select_fusion.bias_g, ...), custom_call_target="tpu_custom_call" | custom-call | tf_op jit(solution)/shard_map/pallas_call | solution.py:1239
  233.1 10.6 %collective-permute-start.10 = (bf16[16,224,128]{2,1,0:T(8,128)(2,1)}, bf16[16,224,128]{2,1,0:T(8,128)(2,1)S(1)}, u32[]{:S(2)}, u32[]{:S(2)}) collective-permute-start(bf16[16,224,128]{2,1,0:T(8,128)(2,1)} %get-tuple-element.92), channel_id=1, source_target_pairs={{0,16},{16,0},{1,17},{17,1},{2,18},{18,2},{3,19},{19,3},{4,20},{20... | collective-permute-start | bytes 2752520 | tf_op jit(solution)/shard_map/ppermute | solution.py:1079
  243.7 4.2 %add_convert_fusion.1 = (bf16[4,2,64,1024]{3,2,1,0:T(8,128)(2,1)S(1)}, bf16[4,2,64,1024]{3,2,1,0:T(8,128)(2,1)}) fusion(bf16[8,2,64,1024]{3,2,1,0:T(8,128)(2,1)} %collective-permute-done.5, bf16[8,2,64,1024]{3,2,1,0:T(8,128)(2,1)} %get-tuple-element.84), kind=kLoop, calls=%fused_computation.1 | loop fusion | flops 4194304 | bytes 6291456 | tf_op jit(solution)/shard_map/convert_element_type | solution.py:1170
  252.5 19.5 %collective-permute-done.11.late_came = bf16[1600,128]{1,0:T(8,128)(2,1)S(1)} collective-permute-done((bf16[1600,128]{1,0:T(8,128)(2,1)}, bf16[1600,128]{1,0:T(8,128)(2,1)S(1)}, u32[]{:S(2)}, u32[]{:S(2)}) %collective-permute-start.11) | collective-permute-done | bytes 409632 | tf_op jit(solution)/shard_map/ppermute | solution.py:1265
  276.7 4.4 %all-to-all-start.3 = ((bf16[16,224,128]{2,1,0:T(8,128)(2,1)}), bf16[16,224,128]{2,1,0:T(8,128)(2,1)}, u32[]{:S(2)}, u32[]{:S(2)}) async-start(bf16[16,224,128]{2,1,0:T(8,128)(2,1)} %shard_map.130), calls=%async_computation.4 | async-start | bytes 1835008 | tf_op jit(solution)/shard_map/all_to_all | solution.py:1271
  285.8 24.3 %collective-permute-done.7 = bf16[2,2,64,1024]{3,2,1,0:T(8,128)(2,1)S(1)} collective-permute-done((bf16[2,2,64,1024]{3,2,1,0:T(8,128)(2,1)}, bf16[2,2,64,1024]{3,2,1,0:T(8,128)(2,1)S(1)}, u32[]{:S(2)}, u32[]{:S(2)}) %collective-permute-start.7) | collective-permute-done | bytes 524320 | tf_op jit(solution)/shard_map/ppermute | solution.py:1165
  313.5 7.9 %shard_map.131 = f32[3120,128]{1,0:T(8,128)} custom-call(s32[12]{0:T(128)} %stack.98.scalars.facts.lengths.here, bf16[16,224,128]{2,1,0:T(8,128)(2,1)} %all-to-all-done.3.got), custom_call_target="tpu_custom_call" | custom-call | tf_op jit(solution)/shard_map/pallas_call | solution.py:1272
  327.9 5.1 %collective-permute-start.9 = (bf16[64,1024]{1,0:T(8,128)(2,1)S(1)}, bf16[64,1024]{1,0:T(8,128)(2,1)S(1)}, u32[]{:S(2)}, u32[]{:S(2)}) collective-permute-start(bf16[64,1024]{1,0:T(8,128)(2,1)S(1)} %get-tuple-element.112), channel_id=1, source_target_pairs={{0,16},{16,0},{1,17},{17,1},{2,18},{18,2},{3,19},{19,3},{4,20},{20... | collective-permute-start | bytes 393224 | tf_op jit(solution)/shard_map/ppermute | solution.py:1079
  333.0 4.4 %add_multiply_fusion = (f32[393632]{0:T(1024)}, f32[393632]{0:T(1024)}, f32[393632]{0:T(1024)}, f32[393632]{0:T(1024)}) fusion(f32[393632]{0:T(1024)S(1)} %copy-done.6, f32[393632]{0:T(1024)S(1)} %copy-done.1, f32[393632]{0:T(1024)} %param.12, f32[1024]{0:T(1024)S(1)} %collective-permute-done.13, f32[4096]{0:T(1024)S(1)} %collective-permute-done.12, ...), kind=kLoop, calls=%fused_computation.4 | loop fusion | flops 3936320 | bytes 12616704 | tf_op jit(solution)/shard_map/add | solution.py:1297
  337.7 45.9 %reduce-scatter.2.cloned.1.call-done = bf16[1,2,64,1024]{3,2,1,0:T(8,128)(2,1)} async-done(((bf16[16,2,64,1024]{3,2,1,0:T(8,128)(2,1)}), bf16[1,2,64,1024]{3,2,1,0:T(8,128)(2,1)}) %reduce-scatter.2.cloned.1.call-update) | async-done | bytes 262160 | tf_op jit(solution)/shard_map/reduce_scatter | solution.py:1211
  (100 shorter events, 58.8 us)
Async XLA Ops:
  7.2 113.8 %all-gather.5.cloned.1.call-start = ((), (), s32[]{:S(2)}) async-start(), calls=%async_computation.6 | async-start | bytes 4456448 | tf_op jit(solution)/shard_map/all_gather | solution.py:1102
  8.4 9.3 %collective-permute-start = (bf16[2,64,1024]{2,1,0:T(8,128)(2,1)S(1)}, bf16[2,64,1024]{2,1,0:T(8,128)(2,1)S(1)}, u32[]{:S(2)}, u32[]{:S(2)}) collective-permute-start(bf16[2,64,1024]{2,1,0:T(8,128)(2,1)S(1)} %get-tuple-element.109), channel_id=1, source_target_pairs={{0,16},{16,0},{1,17},{17,1},{2,18},{18,2},{3,19},{19,3},{4,20},{20... | collective-permute-start | bytes 786440 | tf_op jit(solution)/shard_map/ppermute | solution.py:1079
  18.7 145.9 %all-gather.7.cloned.1.call-start = ((), (), s32[]{:S(2)}) async-start(), calls=%async_computation.7 | async-start | bytes 4456448 | tf_op jit(solution)/shard_map/all_gather | solution.py:1103
  19.4 9.9 %collective-permute-start.2 = (f32[4096]{0:T(1024)S(1)}, f32[4096]{0:T(1024)S(1)}, u32[]{:S(2)}, u32[]{:S(2)}) collective-permute-start(f32[4096]{0:T(1024)S(1)} %slice.68), channel_id=1, source_target_pairs={{1,0},{2,1},{3,2},{4,3},{5,4},{6,5},{7,6},{8,7},{9,8},{10,9},{11,1... | collective-permute-start | bytes 49160 | tf_op jit(solution)/shard_map/ppermute | solution.py:1113
  20.8 8.6 %collective-permute-start.1 = (f32[1024]{0:T(1024)S(1)}, f32[1024]{0:T(1024)S(1)}, u32[]{:S(2)}, u32[]{:S(2)}) collective-permute-start(f32[1024]{0:T(1024)S(1)} %slice.67), channel_id=1, source_target_pairs={{0,1},{1,2},{2,3},{3,4},{4,5},{5,6},{6,7},{7,8},{8,9},{9,10},{10,1... | collective-permute-start | bytes 12296 | tf_op jit(solution)/shard_map/ppermute | solution.py:1112
  88.5 23.4 %copy-start.3 = (bf16[16,240,128]{2,1,0:T(8,128)(2,1)}, bf16[16,240,128]{2,1,0:T(8,128)(2,1)S(1)}, u32[]{:S(2)}) copy-start(bf16[16,240,128]{2,1,0:T(8,128)(2,1)S(1)} %all_to_all.20.own) | copy-start | bytes 2949124
  88.5 23.4 %collective-permute-start.3 = (bf16[16,240,128]{2,1,0:T(8,128)(2,1)S(1)}, bf16[16,240,128]{2,1,0:T(8,128)(2,1)S(1)}, u32[]{:S(2)}, u32[]{:S(2)}) collective-permute-start(bf16[16,240,128]{2,1,0:T(8,128)(2,1)S(1)} %all_to_all.20.own), channel_id=1, source_target_pairs={{0,16},{16,0},{1,17},{17,1},{2,18},{18,2},{3,19},{19,3},{4,20},{20... | collective-permute-start | bytes 2949128 | tf_op jit(solution)/shard_map/ppermute | solution.py:1079
  116.6 33.5 %all-to-all-start.1 = ((bf16[16,160,128]{2,1,0:T(8,128)(2,1)}), bf16[16,160,128]{2,1,0:T(8,128)(2,1)S(1)}, u32[]{:S(2)}, u32[]{:S(2)}) async-start(bf16[16,160,128]{2,1,0:T(8,128)(2,1)} %get-tuple-element.56), calls=%async_computation.1 | async-start | bytes 1310720 | tf_op jit(solution)/shard_map/all_to_all | solution.py:1153
  191.4 17.7 %copy-start.13 = (f32[1,1024]{1,0:T(1,128)S(1)}, f32[1,1024]{1,0:T(1,128)}, u32[]{:S(2)}) copy-start(f32[1,1024]{1,0:T(1,128)} %get-tuple-element.89) | copy-start | bytes 12292
  205.2 38.5 %collective-permute-start.5 = (bf16[8,2,64,1024]{3,2,1,0:T(8,128)(2,1)}, bf16[8,2,64,1024]{3,2,1,0:T(8,128)(2,1)}, u32[]{:S(2)}, u32[]{:S(2)}) collective-permute-start(bf16[8,2,64,1024]{3,2,1,0:T(8,128)(2,1)} %get-tuple-element.85), channel_id=1, source_target_pairs={{0,8},{8,0},{1,9},{9,1},{2,10},{10,2},{3,11},{11,3},{4,12},{12,4},... | collective-permute-start | bytes 6291464 | tf_op jit(solution)/shard_map/ppermute | solution.py:1165
  205.3 22.3 %all-to-all-start.2 = ((bf16[16,160,128]{2,1,0:T(8,128)(2,1)}), bf16[16,160,128]{2,1,0:T(8,128)(2,1)S(1)}, u32[]{:S(2)}, u32[]{:S(2)}) async-start(bf16[16,160,128]{2,1,0:T(8,128)(2,1)} %shard_map.125), calls=%async_computation.3 | async-start | bytes 1310720 | tf_op jit(solution)/shard_map/all_to_all | solution.py:1228
  233.1 38.9 %collective-permute-start.10 = (bf16[16,224,128]{2,1,0:T(8,128)(2,1)}, bf16[16,224,128]{2,1,0:T(8,128)(2,1)S(1)}, u32[]{:S(2)}, u32[]{:S(2)}) collective-permute-start(bf16[16,224,128]{2,1,0:T(8,128)(2,1)} %get-tuple-element.92), channel_id=1, source_target_pairs={{0,16},{16,0},{1,17},{17,1},{2,18},{18,2},{3,19},{19,3},{4,20},{20... | collective-permute-start | bytes 2752520 | tf_op jit(solution)/shard_map/ppermute | solution.py:1079
  247.9 33.7 %collective-permute-start.6 = (bf16[4,2,64,1024]{3,2,1,0:T(8,128)(2,1)}, bf16[4,2,64,1024]{3,2,1,0:T(8,128)(2,1)}, u32[]{:S(2)}, u32[]{:S(2)}) collective-permute-start(bf16[4,2,64,1024]{3,2,1,0:T(8,128)(2,1)} %get-tuple-element.103), channel_id=1, source_target_pairs={{0,1},{1,0},{2,3},{3,2},{4,5},{5,4},{6,7},{7,6},{8,9},{9,8},{10,11... | collective-permute-start | bytes 3145736 | tf_op jit(solution)/shard_map/ppermute | solution.py:1165
  251.2 20.8 %collective-permute-start.11 = (bf16[1600,128]{1,0:T(8,128)(2,1)}, bf16[1600,128]{1,0:T(8,128)(2,1)S(1)}, u32[]{:S(2)}, u32[]{:S(2)}) collective-permute-start(bf16[1600,128]{1,0:T(8,128)(2,1)} %shard_map.129.late), channel_id=1, source_target_pairs={{16,0},{17,1},{18,2},{19,3},{20,4},{21,5},{22,6},{23,7},{24,8},{25... | collective-permute-start | bytes 1228808 | tf_op jit(solution)/shard_map/ppermute | solution.py:1265
  276.7 36.8 %all-to-all-start.3 = ((bf16[16,224,128]{2,1,0:T(8,128)(2,1)}), bf16[16,224,128]{2,1,0:T(8,128)(2,1)}, u32[]{:S(2)}, u32[]{:S(2)}) async-start(bf16[16,224,128]{2,1,0:T(8,128)(2,1)} %shard_map.130), calls=%async_computation.4 | async-start | bytes 1835008 | tf_op jit(solution)/shard_map/all_to_all | solution.py:1271
  281.1 102.4 %reduce-scatter.2.cloned.1.call-start = ((), (), s32[]{:S(2)}) async-start(), calls=%async_computation.5 | async-start | bytes 4456448 | tf_op jit(solution)/shard_map/reduce_scatter | solution.py:1211
  283.9 26.1 %collective-permute-start.7 = (bf16[2,2,64,1024]{3,2,1,0:T(8,128)(2,1)}, bf16[2,2,64,1024]{3,2,1,0:T(8,128)(2,1)S(1)}, u32[]{:S(2)}, u32[]{:S(2)}) collective-permute-start(bf16[2,2,64,1024]{3,2,1,0:T(8,128)(2,1)} %get-tuple-element.105), channel_id=1, source_target_pairs={{0,2},{2,0},{4,6},{6,4},{1,3},{3,1},{5,7},{7,5},{8,10},{10,8},{12,... | collective-permute-start | bytes 1572872 | tf_op jit(solution)/shard_map/ppermute | solution.py:1165
  310.2 17.5 %collective-permute-start.8 = (bf16[1,2,64,1024]{3,2,1,0:T(8,128)(2,1)S(1)}, bf16[1,2,64,1024]{3,2,1,0:T(8,128)(2,1)S(1)}, u32[]{:S(2)}, u32[]{:S(2)}) collective-permute-start(bf16[1,2,64,1024]{3,2,1,0:T(8,128)(2,1)S(1)} %add_convert_fusion.5), channel_id=1, source_target_pairs={{0,4},{4,0},{2,6},{6,2},{1,5},{5,1},{3,7},{7,3},{8,12},{12,8},{10,... | collective-permute-start | bytes 786440 | tf_op jit(solution)/shard_map/ppermute | solution.py:1165
  313.5 19.5 %copy-start.6 = (f32[393632]{0:T(1024)S(1)}, f32[393632]{0:T(1024)}, u32[]{:S(2)}) copy-start(f32[393632]{0:T(1024)} %param.13) | copy-start | bytes 4723588
  322.4 10.6 %collective-permute-start.12 = (f32[4096]{0:T(1024)S(1)}, f32[4096]{0:T(1024)S(1)}, u32[]{:S(2)}, u32[]{:S(2)}) collective-permute-start(f32[4096]{0:T(1024)S(1)} %slice.101), channel_id=1, source_target_pairs={{0,1},{1,2},{2,3},{3,4},{4,5},{5,6},{6,7},{7,8},{8,9},{9,10},{10,1... | collective-permute-start | bytes 49160 | tf_op jit(solution)/shard_map/ppermute | solution.py:1276
  326.4 6.6 %collective-permute-start.13 = (f32[1024]{0:T(1024)S(1)}, f32[1024]{0:T(1024)S(1)}, u32[]{:S(2)}, u32[]{:S(2)}) collective-permute-start(f32[1024]{0:T(1024)S(1)} %slice_bitcast_fusion), channel_id=1, source_target_pairs={{1,0},{2,1},{3,2},{4,3},{5,4},{6,5},{7,6},{8,7},{9,8},{10,9},{11,1... | collective-permute-start | bytes 12296 | tf_op jit(solution)/shard_map/ppermute | solution.py:1277
  327.9 61.7 %copy-start.7 = (bf16[2,64,1024]{2,1,0:T(8,128)(2,1)S(1)}, bf16[2,64,1024]{2,1,0:T(8,128)(2,1)}, u32[]{:S(2)}) copy-start(bf16[2,64,1024]{2,1,0:T(8,128)(2,1)} %param.8) | copy-start | bytes 786436
  327.9 9.5 %collective-permute-start.9 = (bf16[64,1024]{1,0:T(8,128)(2,1)S(1)}, bf16[64,1024]{1,0:T(8,128)(2,1)S(1)}, u32[]{:S(2)}, u32[]{:S(2)}) collective-permute-start(bf16[64,1024]{1,0:T(8,128)(2,1)S(1)} %get-tuple-element.112), channel_id=1, source_target_pairs={{0,16},{16,0},{1,17},{17,1},{2,18},{18,2},{3,19},{19,3},{4,20},{20... | collective-permute-start | bytes 393224 | tf_op jit(solution)/shard_map/ppermute | solution.py:1079
  384.6 5.0 %collective-permute-start.4 = (bf16[64,1024]{1,0:T(8,128)(2,1)S(1)}, bf16[64,1024]{1,0:T(8,128)(2,1)S(1)}, u32[]{:S(2)}, u32[]{:S(2)}) collective-permute-start(bf16[64,1024]{1,0:T(8,128)(2,1)S(1)} %get-tuple-element.115), channel_id=1, source_target_pairs={{0,16},{16,0},{1,17},{17,1},{2,18},{18,2},{3,19},{19,3},{4,20},{20... | collective-permute-start | bytes 393224 | tf_op jit(solution)/shard_map/ppermute | solution.py:1079
  (12 other events, 51.6 us)
Sparse Core Ops, SparseCore 0:
  18.8 68.9 all-gather.4
  90.6 59.8 all-gather.6
  313.6 69.9 reduce-scatter.1
